TPU v7x, 256 devices: a whole 4x4x8 slice. The times are simulated.
256 devices in a mesh: lon: 16 (over y_hi, z), lat: 4 (over x), grp: 4 (over y_lo, core).
Axes of the slice: x: 4, y: 4 (y_hi: 2, y_lo: 2; y = y_hi * 2 + y_lo), z: 8, core: 2. Of those that a mesh axis runs over, the one named last changes fastest.
Arguments:
- sea_surface: float32 [16, 256, 8192], P('grp', 'lat', 'lon'), may hold values from -6 to 6
- velocity: float32 [2, 16, 256, 8192], P(None, 'grp', 'lat', 'lon'), may hold values from -2 to 2
- levels: int32 [256, 8192], P('lat', 'lon'), may hold values from 1 to 50
- wind_basis: bfloat16 [16, 256, 8192], P(None, 'lat', 'lon'), may hold values from -1.5 to 1.5
- proposals: float32 [16, 16], replicated, may hold values from -4 to 4
- member_ids: int32 [16], replicated, may hold values from 0 to 15, each once
- conv_weight: bfloat16 [128, 256], replicated, may hold values from -0.5 to 0.5
- couple_in: float32 [264, 512], replicated, may hold values from -0.375 to 0.375
- couple_in_bias: float32 [512], replicated, may hold values from -3 to 3
- couple_out: float32 [512, 16], replicated, may hold values from -0.25 to 0.25
- couple_out_bias: float32 [16], replicated, may hold values from -3 to 3
Outputs:
- surface_out: float32 [16, 256, 8192], P('grp', 'lat', 'lon')
- velocity_out: float32 [2, 16, 256, 8192], P(None, 'grp', 'lat', 'lon')
- summary: float32 [16, 4, 4, 2, 256], P('lon', 'lat', 'grp')
- weight_step: float32 [176656], replicated
Inputs may be any that keep to these rules, and one draw needn't show every extreme that they name: member_ids is a permutation of 0 to 15.
All inputs are finite; a program needn't handle non-finite values.
Results may differ from a plain program's by a relative error of at most 0.0031.
Values may be sent and summed in bfloat16 or wider, within the bound.
A program may use at most 128 MiB of HBM per device.

v0:
```python
from functools import partial
import math

import jax
import jax.numpy as jnp
from jax import lax
from jax.sharding import PartitionSpec as P

STEPS = 8
NLEV = 50
PH = 8
PW = 16


GRAVITY = 0.45
DRAG_RATE = 0.02
CORI_BASE = 0.05
CORI_SLOPE = 0.1
WIND_SCALE = 0.05
EPSILON = 1e-06
PRECISE = lax.Precision.HIGHEST


def extended(value, sides, width, wrap):
    for axis, dim in sides:
        count, length = (lax.axis_size(axis), value.shape[dim])
        up = [(i, (i + 1) % count) for i in range(count if wrap else count - 1)]
        down = [(j, i) for i, j in up]
        last = lax.slice_in_dim(value, length - width, length, axis=dim)
        initial = lax.slice_in_dim(value, 0, width, axis=dim)
        before = lax.ppermute(last, axis, up)
        after = lax.ppermute(initial, axis, down)
        value = jnp.concatenate([before, value, after], axis=dim)
    return value


def passed_along(value, axis, steps):
    count = lax.axis_size(axis)
    pairs = [(source, (source + steps) % count) for source in range(count)]
    return lax.ppermute(value, axis, pairs)


def from_behind(block, axis, distance):
    devices = range(lax.axis_size(axis))
    route = [(i - distance, i) for i in devices if i - distance in devices]
    return lax.ppermute(block, axis, route)


def to_patches(band_rows, kernel_rows, kernel_cols):
    count, height, breadth = band_rows.shape
    blocks = band_rows.reshape(
        count, height // kernel_rows, kernel_rows, breadth // kernel_cols, kernel_cols
    )
    return blocks.transpose(0, 1, 3, 2, 4).reshape(-1, kernel_rows * kernel_cols)


def flow_loss(params, w_in, b_in, w_out, b_out, summary):
    half_count = params.shape[1] // 2
    lower = params[:, :half_count]
    upper = params[:, half_count:]
    context = jnp.concatenate([lower, summary], axis=1)
    hidden = jnp.tanh(jnp.dot(context, w_in, precision=PRECISE) + b_in)
    out_raw = jnp.dot(hidden, w_out, precision=PRECISE) + b_out
    log_scale = jnp.tanh(out_raw[:, :half_count])
    latent = upper * jnp.exp(log_scale) + out_raw[:, half_count:]
    return jnp.sum(0.5 * latent * latent - log_scale)


def pick_rows(proposals, member_ids, members):
    slot_ids = jnp.arange(member_ids.shape[0], dtype=jnp.int32)
    chosen = jnp.sum(
        jnp.where(members[:, None] == slot_ids[None, :], member_ids[None, :], 0), axis=1
    )
    onehot = (chosen[:, None] == slot_ids[None, :]).astype(jnp.float32)
    return jnp.dot(onehot, proposals, precision=PRECISE)


def depth_rim(sea_depth, rim_width):
    widened = extended(sea_depth, (("lon", 1),), rim_width, True)
    return extended(widened, (("lat", 0),), rim_width, False)


def flow_rim(velocities):
    widened = extended(velocities, (("lon", 3),), 1, True)
    return extended(widened, (("lat", 2),), 1, False)


def level_lower(new_level):
    west_edge = passed_along(new_level[:, :, -1:], "lon", 1)
    south_edge = from_behind(new_level[:, -1:, :], "lat", 1)
    west_level = jnp.concatenate([west_edge, new_level[:, :, :-1]], axis=2)
    south_level = jnp.concatenate([south_edge, new_level[:, :-1, :]], axis=1)
    return (west_level, south_level)


def velocity_update(
    east_flow,
    north_flow,
    east_wide,
    north_wide,
    new_level,
    west_level,
    south_level,
    cori_u,
    cori_v,
    forcing,
):
    v_mean = 0.25 * (
        north_wide[:, 1:-1, 1:-1]
        + north_wide[:, 2:, 1:-1]
        + north_wide[:, 1:-1, :-2]
        + north_wide[:, 2:, :-2]
    )
    u_mean = 0.25 * (
        east_wide[:, 1:-1, 1:-1]
        + east_wide[:, 1:-1, 2:]
        + east_wide[:, :-2, 1:-1]
        + east_wide[:, :-2, 2:]
    )
    new_east = (
        east_flow
        + cori_u * v_mean
        - GRAVITY * (new_level - west_level)
        - DRAG_RATE * east_flow
        + forcing
    )
    new_north = (
        north_flow - cori_v * u_mean - GRAVITY * (new_level - south_level) - DRAG_RATE * north_flow
    )
    return (new_east, new_north)


def shards(
    sea_surface,
    velocity,
    levels,
    wind_basis,
    proposals,
    member_ids,
    conv_weight,
    couple_in,
    couple_in_bias,
    couple_out,
    couple_out_bias,
):
    members_here, tile_rows, tile_cols = sea_surface.shape
    lat_count = lax.axis_size("lat")
    lon_count = lax.axis_size("lon")
    lat_index = lax.axis_index("lat")
    lon_index = lax.axis_index("lon")
    grp_index = lax.axis_index("grp")
    total_rows = tile_rows * lat_count
    total_cols = tile_cols * lon_count
    sea_depth = levels.astype(jnp.float32) / NLEV
    rim_width = 1
    depth_wide = depth_rim(sea_depth, rim_width)
    row_index = (lat_index * tile_rows + jnp.arange(tile_rows, dtype=jnp.int32)).astype(
        jnp.float32
    )[:, None]
    cori_u = CORI_BASE + CORI_SLOPE * (row_index + 0.5) / total_rows
    cori_v = CORI_BASE + CORI_SLOPE * row_index / total_rows
    local_members = grp_index * members_here + jnp.arange(members_here, dtype=jnp.int32)
    coeff_rows = pick_rows(proposals, member_ids, local_members).astype(jnp.bfloat16)
    forcing = WIND_SCALE * jnp.dot(
        coeff_rows, wind_basis.reshape(wind_basis.shape[0], -1), preferred_element_type=jnp.float32
    ).reshape(members_here, tile_rows, tile_cols)
    sea_level, east_flow, north_flow = (sea_surface, velocity[0], velocity[1])
    frames = []
    hu_face = 0.5 * (depth_wide[1:-1, 1:] + depth_wide[1:-1, :-1])
    hv_face = 0.5 * (depth_wide[1:, 1:-1] + depth_wide[:-1, 1:-1])
    for step_index in range(STEPS):
        velocities = flow_rim(jnp.stack([east_flow, north_flow]))
        east_wide, north_wide = (velocities[0], velocities[1])
        flux_x = hu_face * east_wide[:, 1:-1, 1:]
        flux_y = hv_face * north_wide[:, 1:, 1:-1]
        new_level = sea_level - (
            flux_x[:, :, 1:] - flux_x[:, :, :-1] + flux_y[:, 1:, :] - flux_y[:, :-1, :]
        )
        west_level, south_level = level_lower(new_level)
        east_flow, north_flow = velocity_update(
            east_flow,
            north_flow,
            east_wide,
            north_wide,
            new_level,
            west_level,
            south_level,
            cori_u,
            cori_v,
            forcing,
        )
        sea_level = new_level
        frames.append(sea_level.astype(jnp.bfloat16))
    frames = jnp.stack(frames)
    all_items = frames.shape[0] * members_here
    item_count = all_items // lon_count
    feat_count = conv_weight.shape[1]
    inv_root = 1.0 / math.sqrt(tile_rows // PH * (total_cols // PW))
    item_ids = lon_index * item_count + jnp.arange(item_count, dtype=jnp.int32)
    sample_members = grp_index * members_here + item_ids % members_here
    params = pick_rows(proposals, member_ids, sample_members)
    loss_fn = partial(flow_loss, params)
    blocks = frames.reshape(lon_count, item_count, tile_rows, tile_cols)
    band_rows = lax.all_to_all(blocks, "lon", split_axis=0, concat_axis=3, tiled=True)[0]
    patch_rows = to_patches(band_rows, PH, PW)
    activation = jnp.tanh(
        jnp.dot(patch_rows, conv_weight, preferred_element_type=jnp.float32)
    ).reshape(item_count, -1, feat_count)
    summary = jnp.sum(activation, axis=1) * inv_root
    loss_value, pullback = jax.vjp(
        loss_fn, couple_in, couple_in_bias, couple_out, couple_out_bias, summary
    )
    g_in, g_in_b, g_out, g_out_b, d_summary = pullback(jnp.ones_like(loss_value))
    d_pre = (
        ((d_summary * inv_root)[:, None, :] * (1.0 - activation * activation))
        .astype(jnp.bfloat16)
        .reshape(-1, feat_count)
    )
    g_conv = lax.dot_general(
        patch_rows, d_pre, (((0,), (0,)), ((), ())), preferred_element_type=jnp.float32
    )
    grad_local = jnp.concatenate(
        [g_conv.reshape(-1), g_in.reshape(-1), g_in_b, g_out.reshape(-1), g_out_b]
    )
    grad_total = lax.psum(grad_local, ("lon", "lat", "grp"))
    weight_step = -grad_total / jnp.sqrt(jnp.mean(grad_total * grad_total) + EPSILON)
    return (
        sea_level,
        jnp.stack([east_flow, north_flow]),
        summary.reshape(1, 1, 1, item_count, feat_count),
        weight_step,
    )


def solution(mesh):
    in_specs = (
        P("grp", "lat", "lon"),
        P(None, "grp", "lat", "lon"),
        P("lat", "lon"),
        P(None, "lat", "lon"),
        P(),
        P(),
        P(),
        P(),
        P(),
        P(),
        P(),
    )
    out_specs = (
        P("grp", "lat", "lon"),
        P(None, "grp", "lat", "lon"),
        P("lon", "lat", "grp", None, None),
        P(),
    )
    return jax.shard_map(shards, mesh=mesh, in_specs=in_specs, out_specs=out_specs, check_vma=False)
```

profile of v0, /device:TPU:1, one launch (start us, length us, event | category | flops | bytes accessed | tf_op | source)
XLA Modules:
  0.0 651.2 jit_solution(2624770752842426924)
XLA Ops:
  8.2 2.5 collective-permute-start.1
  10.7 6.7 %collective-permute-start = (f32[64,1]{1,0:T(8,128)S(1)}, f32[64,1]{1,0:T(8,128)S(1)}, u32[]{:S(2)}, u32[]{:S(2)}) collective-permute-start(f32[64,1]{1,0:T(8,128)S(1)} %get-tuple-element.101), channel_id=1, source_target_pairs={{16,0},{32,16},{48,32},{64,48},{80,64},{96,80},{112,96},{128,112},... | collective-permute-start | bytes 776 | tf_op jit(solution)/shard_map/ppermute | solution.py:32
  19.6 5.1 collective-permute-start.3
  26.4 4.0 collective-permute-start.7
  30.6 3.1 collective-permute-start.4
  35.2 3.1 collective-permute-done.5
  41.3 3.1 collective-permute-start.9
  44.5 7.4 %collective-permute-done.8 = f32[4,64,1]{2,0,1:T(4,128)S(1)} collective-permute-done((f32[4,64,1]{2,0,1:T(4,128)S(1)}, f32[4,64,1]{2,0,1:T(4,128)S(1)}, u32[]{:S(2)}, u32[]{:S(2)}) %collective-permute-start.8) | collective-permute-done | bytes 1056 | tf_op jit(solution)/shard_map/ppermute | solution.py:40
  51.9 2.5 fusion.85
  54.7 5.1 collective-permute-start.11
  59.7 3.8 collective-permute-done.10
  63.6 2.7 collective-permute-start.12
  67.8 3.0 collective-permute-done.13
  73.1 1.9 collective-permute-start.15
  75.3 7.4 %collective-permute-done.14 = f32[4,64,1]{2,0,1:T(4,128)S(1)} collective-permute-done((f32[4,64,1]{2,0,1:T(4,128)S(1)}, f32[4,64,1]{2,0,1:T(4,128)S(1)}, u32[]{:S(2)}, u32[]{:S(2)}) %collective-permute-start.14) | collective-permute-done | bytes 1056 | tf_op jit(solution)/shard_map/ppermute | solution.py:40
  82.7 2.3 fusion.75
  85.3 5.1 collective-permute-start.17
  90.4 3.8 collective-permute-done.16
  94.2 1.9 collective-permute-start.18
  97.5 3.5 collective-permute-done.19
  103.3 1.9 collective-permute-start.21
  105.5 7.4 %collective-permute-done.20 = f32[4,64,1]{2,0,1:T(4,128)S(1)} collective-permute-done((f32[4,64,1]{2,0,1:T(4,128)S(1)}, f32[4,64,1]{2,0,1:T(4,128)S(1)}, u32[]{:S(2)}, u32[]{:S(2)}) %collective-permute-start.20) | collective-permute-done | bytes 1056 | tf_op jit(solution)/shard_map/ppermute | solution.py:40
  112.9 2.3 fusion.65
  115.5 5.1 collective-permute-start.23
  120.6 5.2 collective-permute-done.22
  125.8 2.4 collective-permute-start.24
  129.5 3.5 collective-permute-done.25
  135.4 1.9 collective-permute-start.27
  137.6 7.4 %collective-permute-done.26 = f32[4,64,1]{2,0,1:T(4,128)S(1)} collective-permute-done((f32[4,64,1]{2,0,1:T(4,128)S(1)}, f32[4,64,1]{2,0,1:T(4,128)S(1)}, u32[]{:S(2)}, u32[]{:S(2)}) %collective-permute-start.26) | collective-permute-done | bytes 1056 | tf_op jit(solution)/shard_map/ppermute | solution.py:40
  144.9 2.3 fusion.55
  147.6 5.1 collective-permute-start.29
  152.6 3.8 collective-permute-done.28
  156.5 1.9 collective-permute-start.30
  159.7 3.2 collective-permute-done.31
  165.2 1.9 collective-permute-start.33
  167.4 7.7 %collective-permute-done.32 = f32[4,64,1]{2,0,1:T(4,128)S(1)} collective-permute-done((f32[4,64,1]{2,0,1:T(4,128)S(1)}, f32[4,64,1]{2,0,1:T(4,128)S(1)}, u32[]{:S(2)}, u32[]{:S(2)}) %collective-permute-start.32) | collective-permute-done | bytes 1056 | tf_op jit(solution)/shard_map/ppermute | solution.py:40
  175.1 2.3 fusion.45
  177.7 5.2 collective-permute-start.35
  183.0 3.6 collective-permute-done.34
  186.7 1.9 collective-permute-start.36
  189.9 3.2 collective-permute-done.37
  195.4 1.9 collective-permute-start.39
  197.6 8.4 %collective-permute-done.38 = f32[4,64,1]{2,0,1:T(4,128)S(1)} collective-permute-done((f32[4,64,1]{2,0,1:T(4,128)S(1)}, f32[4,64,1]{2,0,1:T(4,128)S(1)}, u32[]{:S(2)}, u32[]{:S(2)}) %collective-permute-start.38) | collective-permute-done | bytes 1056 | tf_op jit(solution)/shard_map/ppermute | solution.py:40
  206.0 2.3 fusion.35
  208.6 5.1 collective-permute-start.41
  213.7 3.8 collective-permute-done.40
  220.5 3.2 collective-permute-done.43
  226.0 2.2 collective-permute-start.45
  228.5 7.9 %collective-permute-done.44 = f32[4,64,1]{2,0,1:T(4,128)S(1)} collective-permute-done((f32[4,64,1]{2,0,1:T(4,128)S(1)}, f32[4,64,1]{2,0,1:T(4,128)S(1)}, u32[]{:S(2)}, u32[]{:S(2)}) %collective-permute-start.44) | collective-permute-done | bytes 1056 | tf_op jit(solution)/shard_map/ppermute | solution.py:40
  236.4 2.3 fusion.25
  239.1 5.1 collective-permute-start.47
  244.1 3.8 collective-permute-done.46
  248.0 2.2 collective-permute-start.48
  251.5 3.2 collective-permute-done.49
  259.0 6.8 %all-to-all-start = ((bf16[16,2,64,512]{3,2,1,0:T(8,128)(2,1)}), bf16[16,2,64,512]{3,2,1,0:T(8,128)(2,1)}, u32[]{:S(2)}, u32[]{:S(2)}) async-start(bf16[16,2,64,512]{3,2,1,0:T(8,128)(2,1)} %bitcast.187), calls=%async_computation | async-start | bytes 4194304 | tf_op jit(solution)/shard_map/all_to_all | solution.py:204
  269.4 2.5 collective-permute-start.51
  273.4 21.5 %all-to-all-done = bf16[16,2,64,512]{3,2,1,0:T(8,128)(2,1)} async-done(((bf16[16,2,64,512]{3,2,1,0:T(8,128)(2,1)}), bf16[16,2,64,512]{3,2,1,0:T(8,128)(2,1)}, u32[]{:S(2)}, u32[]{:S(2)}) %all-to-all-start) | async-done | bytes 2097184 | tf_op jit(solution)/shard_map/all_to_all | solution.py:204
  294.9 2.8 copy.44
  297.6 15.5 %reshape_squeeze.3 = bf16[2,8,8,512,16]{4,3,2,1,0:T(8,128)(2,1)} reshape(bf16[1,2,64,16,512]{4,3,2,1,0:T(8,128)(2,1)S(1)} %copy.44) | data formatting | bytes 4194304 | tf_op jit(solution)/shard_map/reshape;squeeze | solution.py:51
  313.1 14.9 %copy.45 = bf16[2,8,512,8,16]{2,1,0,4,3:T(8,128)(2,1)} copy(bf16[2,8,512,8,16]{4,2,3,1,0:T(8,128)(2,1)} %bitcast.137) | data formatting | bytes 4194304 | tf_op jit(solution)/shard_map/transpose | solution.py:54
  328.0 2.9 reshape.101
  350.0 3.3 fusion.15
  354.8 284.6 %all-reduce.4.cloned.1.call-done = f32[176656]{0:T(1024)} async-done(((f32[176656]{0:T(1024)}), f32[176656]{0:T(1024)}) %all-reduce.4.cloned.1.call-update) | async-done | bytes 706640 | tf_op jit(solution)/shard_map/psum | solution.py:225
  642.0 2.0 negate_divide_fusion
  (214 shorter events, 70.0 us)
Async XLA Ops:
  7.2 323.7 %copy-start = (bf16[128,256]{1,0:T(8,128)(2,1)S(1)}, bf16[128,256]{1,0:T(8,128)(2,1)}, u32[]{:S(2)}) copy-start(bf16[128,256]{1,0:T(8,128)(2,1)} %param.17) | copy-start | bytes 196612
  8.2 16.8 %collective-permute-start.1 = (f32[64,1]{1,0:T(8,128)S(1)}, f32[64,1]{1,0:T(8,128)S(1)}, u32[]{:S(2)}, u32[]{:S(2)}) collective-permute-start(f32[64,1]{1,0:T(8,128)S(1)} %get-tuple-element.100), channel_id=1, source_target_pairs={{0,16},{16,32},{32,48},{48,64},{64,80},{80,96},{96,112},{112,128},... | collective-permute-start | bytes 776 | tf_op jit(solution)/shard_map/ppermute | solution.py:31
  10.7 13.9 %copy-start.18 = (s32[16]{0:T(128)S(1)}, s32[16]{0:T(128)}, u32[]{:S(2)}) copy-start(s32[16]{0:T(128)} %param.16) | copy-start | bytes 196
  10.7 14.1 %copy-start.17 = (f32[16,16]{1,0:T(8,128)S(1)}, f32[16,16]{1,0:T(8,128)}, u32[]{:S(2)}) copy-start(f32[16,16]{1,0:T(8,128)} %param.15) | copy-start | bytes 3076
  10.7 14.3 %collective-permute-start = (f32[64,1]{1,0:T(8,128)S(1)}, f32[64,1]{1,0:T(8,128)S(1)}, u32[]{:S(2)}, u32[]{:S(2)}) collective-permute-start(f32[64,1]{1,0:T(8,128)S(1)} %get-tuple-element.101), channel_id=1, source_target_pairs={{16,0},{32,16},{48,32},{64,48},{80,64},{96,80},{112,96},{128,112},... | collective-permute-start | bytes 776 | tf_op jit(solution)/shard_map/ppermute | solution.py:32
  19.5 11.0 %collective-permute-start.2 = (f32[2,4,64,1]{3,1,2,0:T(4,128)S(1)}, f32[2,4,64,1]{3,1,2,0:T(4,128)S(1)}, u32[]{:S(2)}, u32[]{:S(2)}) collective-permute-start(f32[2,4,64,1]{3,1,2,0:T(4,128)S(1)} %get-tuple-element.82), channel_id=1, source_target_pairs={{0,16},{16,32},{32,48},{48,64},{64,80},{80,96},{96,112},{112,128},... | collective-permute-start | bytes 6152 | tf_op jit(solution)/shard_map/ppermute | solution.py:31
  19.6 11.0 %collective-permute-start.3 = (f32[2,4,64,1]{3,1,2,0:T(4,128)S(1)}, f32[2,4,64,1]{3,1,2,0:T(4,128)S(1)}, u32[]{:S(2)}, u32[]{:S(2)}) collective-permute-start(f32[2,4,64,1]{3,1,2,0:T(4,128)S(1)} %get-tuple-element.83), channel_id=1, source_target_pairs={{16,0},{32,16},{48,32},{64,48},{80,64},{96,80},{112,96},{128,112},... | collective-permute-start | bytes 6152 | tf_op jit(solution)/shard_map/ppermute | solution.py:32
  25.1 10.0 %collective-permute-start.6 = (f32[1,514]{1,0:T(1,128)S(1)}, f32[1,514]{1,0:T(1,128)S(1)}, u32[]{:S(2)}, u32[]{:S(2)}) collective-permute-start(f32[1,514]{1,0:T(1,128)S(1)} %get-tuple-element.98), channel_id=1, source_target_pairs={{4,0},{8,4},{12,8},{5,1},{9,5},{13,9},{6,2},{10,6},{14,10},{7,3},{... | collective-permute-start | bytes 6176 | tf_op jit(solution)/shard_map/ppermute | solution.py:32
  26.4 8.7 %collective-permute-start.7 = (f32[1,514]{1,0:T(1,128)S(1)}, f32[1,514]{1,0:T(1,128)S(1)}, u32[]{:S(2)}, u32[]{:S(2)}) collective-permute-start(f32[1,514]{1,0:T(1,128)S(1)} %get-tuple-element.99), channel_id=1, source_target_pairs={{0,4},{4,8},{8,12},{1,5},{5,9},{9,13},{2,6},{6,10},{10,14},{3,7},{... | collective-permute-start | bytes 6176 | tf_op jit(solution)/shard_map/ppermute | solution.py:31
  30.6 4.6 collective-permute-start.4
  33.7 4.5 collective-permute-start.5
  40.4 11.5 %copy-start.16 = (bf16[16,64,512]{2,1,0:T(8,128)(2,1)S(1)}, bf16[16,64,512]{2,1,0:T(8,128)(2,1)}, u32[]{:S(2)}) copy-start(bf16[16,64,512]{2,1,0:T(8,128)(2,1)} %param.14) | copy-start | bytes 3145732
  41.3 10.6 %collective-permute-start.9 = (f32[4,1,512]{2,0,1:T(4,128)S(1)}, f32[4,1,512]{2,0,1:T(4,128)S(1)}, u32[]{:S(2)}, u32[]{:S(2)}) collective-permute-start(f32[4,1,512]{2,0,1:T(4,128)S(1)} %slice.849), channel_id=1, source_target_pairs={{0,4},{4,8},{8,12},{1,5},{5,9},{9,13},{2,6},{6,10},{10,14},{3,7},{... | collective-permute-start | bytes 24584 | tf_op jit(solution)/shard_map/ppermute | solution.py:46
  44.4 7.5 %collective-permute-start.8 = (f32[4,64,1]{2,0,1:T(4,128)S(1)}, f32[4,64,1]{2,0,1:T(4,128)S(1)}, u32[]{:S(2)}, u32[]{:S(2)}) collective-permute-start(f32[4,64,1]{2,0,1:T(4,128)S(1)} %slice.842), channel_id=1, source_target_pairs={{0,16},{16,32},{32,48},{48,64},{64,80},{80,96},{96,112},{112,128},... | collective-permute-start | bytes 3080 | tf_op jit(solution)/shard_map/ppermute | solution.py:40
  54.6 8.9 %collective-permute-start.10 = (f32[2,4,64,1]{3,1,2,0:T(4,128)S(1)}, f32[2,4,64,1]{3,1,2,0:T(4,128)S(1)}, u32[]{:S(2)}, u32[]{:S(2)}) collective-permute-start(f32[2,4,64,1]{3,1,2,0:T(4,128)S(1)} %get-tuple-element.80), channel_id=1, source_target_pairs={{0,16},{16,32},{32,48},{48,64},{64,80},{80,96},{96,112},{112,128},... | collective-permute-start | bytes 6152 | tf_op jit(solution)/shard_map/ppermute | solution.py:31
  54.7 8.8 %collective-permute-start.11 = (f32[2,4,64,1]{3,1,2,0:T(4,128)S(1)}, f32[2,4,64,1]{3,1,2,0:T(4,128)S(1)}, u32[]{:S(2)}, u32[]{:S(2)}) collective-permute-start(f32[2,4,64,1]{3,1,2,0:T(4,128)S(1)} %get-tuple-element.81), channel_id=1, source_target_pairs={{16,0},{32,16},{48,32},{64,48},{80,64},{96,80},{112,96},{128,112},... | collective-permute-start | bytes 6152 | tf_op jit(solution)/shard_map/ppermute | solution.py:32
  63.6 4.2 collective-permute-start.12
  66.3 4.5 collective-permute-start.13
  73.1 9.6 %collective-permute-start.15 = (f32[4,1,512]{2,0,1:T(4,128)S(1)}, f32[4,1,512]{2,0,1:T(4,128)S(1)}, u32[]{:S(2)}, u32[]{:S(2)}) collective-permute-start(f32[4,1,512]{2,0,1:T(4,128)S(1)} %slice.869), channel_id=1, source_target_pairs={{0,4},{4,8},{8,12},{1,5},{5,9},{9,13},{2,6},{6,10},{10,14},{3,7},{... | collective-permute-start | bytes 24584 | tf_op jit(solution)/shard_map/ppermute | solution.py:46
  75.2 7.5 %collective-permute-start.14 = (f32[4,64,1]{2,0,1:T(4,128)S(1)}, f32[4,64,1]{2,0,1:T(4,128)S(1)}, u32[]{:S(2)}, u32[]{:S(2)}) collective-permute-start(f32[4,64,1]{2,0,1:T(4,128)S(1)} %slice.863), channel_id=1, source_target_pairs={{0,16},{16,32},{32,48},{48,64},{64,80},{80,96},{96,112},{112,128},... | collective-permute-start | bytes 3080 | tf_op jit(solution)/shard_map/ppermute | solution.py:40
  85.2 8.9 %collective-permute-start.16 = (f32[2,4,64,1]{3,1,2,0:T(4,128)S(1)}, f32[2,4,64,1]{3,1,2,0:T(4,128)S(1)}, u32[]{:S(2)}, u32[]{:S(2)}) collective-permute-start(f32[2,4,64,1]{3,1,2,0:T(4,128)S(1)} %get-tuple-element.78), channel_id=1, source_target_pairs={{0,16},{16,32},{32,48},{48,64},{64,80},{80,96},{96,112},{112,128},... | collective-permute-start | bytes 6152 | tf_op jit(solution)/shard_map/ppermute | solution.py:31
  85.3 8.8 %collective-permute-start.17 = (f32[2,4,64,1]{3,1,2,0:T(4,128)S(1)}, f32[2,4,64,1]{3,1,2,0:T(4,128)S(1)}, u32[]{:S(2)}, u32[]{:S(2)}) collective-permute-start(f32[2,4,64,1]{3,1,2,0:T(4,128)S(1)} %get-tuple-element.79), channel_id=1, source_target_pairs={{16,0},{32,16},{48,32},{64,48},{80,64},{96,80},{112,96},{128,112},... | collective-permute-start | bytes 6152 | tf_op jit(solution)/shard_map/ppermute | solution.py:32
  94.2 3.2 collective-permute-start.18
  96.2 4.8 collective-permute-start.19
  103.3 9.6 %collective-permute-start.21 = (f32[4,1,512]{2,0,1:T(4,128)S(1)}, f32[4,1,512]{2,0,1:T(4,128)S(1)}, u32[]{:S(2)}, u32[]{:S(2)}) collective-permute-start(f32[4,1,512]{2,0,1:T(4,128)S(1)} %slice.889), channel_id=1, source_target_pairs={{0,4},{4,8},{8,12},{1,5},{5,9},{9,13},{2,6},{6,10},{10,14},{3,7},{... | collective-permute-start | bytes 24584 | tf_op jit(solution)/shard_map/ppermute | solution.py:46
  105.4 7.5 %collective-permute-start.20 = (f32[4,64,1]{2,0,1:T(4,128)S(1)}, f32[4,64,1]{2,0,1:T(4,128)S(1)}, u32[]{:S(2)}, u32[]{:S(2)}) collective-permute-start(f32[4,64,1]{2,0,1:T(4,128)S(1)} %slice.883), channel_id=1, source_target_pairs={{0,16},{16,32},{32,48},{48,64},{64,80},{80,96},{96,112},{112,128},... | collective-permute-start | bytes 3080 | tf_op jit(solution)/shard_map/ppermute | solution.py:40
  115.4 10.3 %collective-permute-start.22 = (f32[2,4,64,1]{3,1,2,0:T(4,128)S(1)}, f32[2,4,64,1]{3,1,2,0:T(4,128)S(1)}, u32[]{:S(2)}, u32[]{:S(2)}) collective-permute-start(f32[2,4,64,1]{3,1,2,0:T(4,128)S(1)} %get-tuple-element.76), channel_id=1, source_target_pairs={{0,16},{16,32},{32,48},{48,64},{64,80},{80,96},{96,112},{112,128},... | collective-permute-start | bytes 6152 | tf_op jit(solution)/shard_map/ppermute | solution.py:31
  115.5 10.2 %collective-permute-start.23 = (f32[2,4,64,1]{3,1,2,0:T(4,128)S(1)}, f32[2,4,64,1]{3,1,2,0:T(4,128)S(1)}, u32[]{:S(2)}, u32[]{:S(2)}) collective-permute-start(f32[2,4,64,1]{3,1,2,0:T(4,128)S(1)} %get-tuple-element.77), channel_id=1, source_target_pairs={{16,0},{32,16},{48,32},{64,48},{80,64},{96,80},{112,96},{128,112},... | collective-permute-start | bytes 6152 | tf_op jit(solution)/shard_map/ppermute | solution.py:32
  125.8 3.7 collective-permute-start.24
  128.2 4.8 collective-permute-start.25
  135.4 9.6 %collective-permute-start.27 = (f32[4,1,512]{2,0,1:T(4,128)S(1)}, f32[4,1,512]{2,0,1:T(4,128)S(1)}, u32[]{:S(2)}, u32[]{:S(2)}) collective-permute-start(f32[4,1,512]{2,0,1:T(4,128)S(1)} %slice.909), channel_id=1, source_target_pairs={{0,4},{4,8},{8,12},{1,5},{5,9},{9,13},{2,6},{6,10},{10,14},{3,7},{... | collective-permute-start | bytes 24584 | tf_op jit(solution)/shard_map/ppermute | solution.py:46
  137.4 7.5 %collective-permute-start.26 = (f32[4,64,1]{2,0,1:T(4,128)S(1)}, f32[4,64,1]{2,0,1:T(4,128)S(1)}, u32[]{:S(2)}, u32[]{:S(2)}) collective-permute-start(f32[4,64,1]{2,0,1:T(4,128)S(1)} %slice.903), channel_id=1, source_target_pairs={{0,16},{16,32},{32,48},{48,64},{64,80},{80,96},{96,112},{112,128},... | collective-permute-start | bytes 3080 | tf_op jit(solution)/shard_map/ppermute | solution.py:40
  147.5 8.9 %collective-permute-start.28 = (f32[2,4,64,1]{3,1,2,0:T(4,128)S(1)}, f32[2,4,64,1]{3,1,2,0:T(4,128)S(1)}, u32[]{:S(2)}, u32[]{:S(2)}) collective-permute-start(f32[2,4,64,1]{3,1,2,0:T(4,128)S(1)} %get-tuple-element.74), channel_id=1, source_target_pairs={{0,16},{16,32},{32,48},{48,64},{64,80},{80,96},{96,112},{112,128},... | collective-permute-start | bytes 6152 | tf_op jit(solution)/shard_map/ppermute | solution.py:31
  147.6 8.8 %collective-permute-start.29 = (f32[2,4,64,1]{3,1,2,0:T(4,128)S(1)}, f32[2,4,64,1]{3,1,2,0:T(4,128)S(1)}, u32[]{:S(2)}, u32[]{:S(2)}) collective-permute-start(f32[2,4,64,1]{3,1,2,0:T(4,128)S(1)} %get-tuple-element.75), channel_id=1, source_target_pairs={{16,0},{32,16},{48,32},{64,48},{80,64},{96,80},{112,96},{128,112},... | collective-permute-start | bytes 6152 | tf_op jit(solution)/shard_map/ppermute | solution.py:32
  156.5 3.2 collective-permute-start.30
  158.4 4.5 collective-permute-start.31
  165.2 9.9 %collective-permute-start.33 = (f32[4,1,512]{2,0,1:T(4,128)S(1)}, f32[4,1,512]{2,0,1:T(4,128)S(1)}, u32[]{:S(2)}, u32[]{:S(2)}) collective-permute-start(f32[4,1,512]{2,0,1:T(4,128)S(1)} %slice.929), channel_id=1, source_target_pairs={{0,4},{4,8},{8,12},{1,5},{5,9},{9,13},{2,6},{6,10},{10,14},{3,7},{... | collective-permute-start | bytes 24584 | tf_op jit(solution)/shard_map/ppermute | solution.py:46
  167.3 7.8 %collective-permute-start.32 = (f32[4,64,1]{2,0,1:T(4,128)S(1)}, f32[4,64,1]{2,0,1:T(4,128)S(1)}, u32[]{:S(2)}, u32[]{:S(2)}) collective-permute-start(f32[4,64,1]{2,0,1:T(4,128)S(1)} %slice.923), channel_id=1, source_target_pairs={{0,16},{16,32},{32,48},{48,64},{64,80},{80,96},{96,112},{112,128},... | collective-permute-start | bytes 3080 | tf_op jit(solution)/shard_map/ppermute | solution.py:40
  177.7 8.9 %collective-permute-start.34 = (f32[2,4,64,1]{3,1,2,0:T(4,128)S(1)}, f32[2,4,64,1]{3,1,2,0:T(4,128)S(1)}, u32[]{:S(2)}, u32[]{:S(2)}) collective-permute-start(f32[2,4,64,1]{3,1,2,0:T(4,128)S(1)} %get-tuple-element.72), channel_id=1, source_target_pairs={{0,16},{16,32},{32,48},{48,64},{64,80},{80,96},{96,112},{112,128},... | collective-permute-start | bytes 6152 | tf_op jit(solution)/shard_map/ppermute | solution.py:31
  177.7 8.8 %collective-permute-start.35 = (f32[2,4,64,1]{3,1,2,0:T(4,128)S(1)}, f32[2,4,64,1]{3,1,2,0:T(4,128)S(1)}, u32[]{:S(2)}, u32[]{:S(2)}) collective-permute-start(f32[2,4,64,1]{3,1,2,0:T(4,128)S(1)} %get-tuple-element.73), channel_id=1, source_target_pairs={{16,0},{32,16},{48,32},{64,48},{80,64},{96,80},{112,96},{128,112},... | collective-permute-start | bytes 6152 | tf_op jit(solution)/shard_map/ppermute | solution.py:32
  186.7 3.2 collective-permute-start.36
  188.6 4.5 collective-permute-start.37
  195.4 10.6 %collective-permute-start.39 = (f32[4,1,512]{2,0,1:T(4,128)S(1)}, f32[4,1,512]{2,0,1:T(4,128)S(1)}, u32[]{:S(2)}, u32[]{:S(2)}) collective-permute-start(f32[4,1,512]{2,0,1:T(4,128)S(1)} %slice.949), channel_id=1, source_target_pairs={{0,4},{4,8},{8,12},{1,5},{5,9},{9,13},{2,6},{6,10},{10,14},{3,7},{... | collective-permute-start | bytes 24584 | tf_op jit(solution)/shard_map/ppermute | solution.py:46
  197.5 8.5 %collective-permute-start.38 = (f32[4,64,1]{2,0,1:T(4,128)S(1)}, f32[4,64,1]{2,0,1:T(4,128)S(1)}, u32[]{:S(2)}, u32[]{:S(2)}) collective-permute-start(f32[4,64,1]{2,0,1:T(4,128)S(1)} %slice.943), channel_id=1, source_target_pairs={{0,16},{16,32},{32,48},{48,64},{64,80},{80,96},{96,112},{112,128},... | collective-permute-start | bytes 3080 | tf_op jit(solution)/shard_map/ppermute | solution.py:40
  208.5 8.9 %collective-permute-start.40 = (f32[2,4,64,1]{3,1,2,0:T(4,128)S(1)}, f32[2,4,64,1]{3,1,2,0:T(4,128)S(1)}, u32[]{:S(2)}, u32[]{:S(2)}) collective-permute-start(f32[2,4,64,1]{3,1,2,0:T(4,128)S(1)} %get-tuple-element.70), channel_id=1, source_target_pairs={{0,16},{16,32},{32,48},{48,64},{64,80},{80,96},{96,112},{112,128},... | collective-permute-start | bytes 6152 | tf_op jit(solution)/shard_map/ppermute | solution.py:31
  208.6 8.8 %collective-permute-start.41 = (f32[2,4,64,1]{3,1,2,0:T(4,128)S(1)}, f32[2,4,64,1]{3,1,2,0:T(4,128)S(1)}, u32[]{:S(2)}, u32[]{:S(2)}) collective-permute-start(f32[2,4,64,1]{3,1,2,0:T(4,128)S(1)} %get-tuple-element.71), channel_id=1, source_target_pairs={{16,0},{32,16},{48,32},{64,48},{80,64},{96,80},{112,96},{128,112},... | collective-permute-start | bytes 6152 | tf_op jit(solution)/shard_map/ppermute | solution.py:32
  217.5 3.0 collective-permute-start.42
  219.2 4.5 collective-permute-start.43
  226.0 10.4 %collective-permute-start.45 = (f32[4,1,512]{2,0,1:T(4,128)S(1)}, f32[4,1,512]{2,0,1:T(4,128)S(1)}, u32[]{:S(2)}, u32[]{:S(2)}) collective-permute-start(f32[4,1,512]{2,0,1:T(4,128)S(1)} %slice.969), channel_id=1, source_target_pairs={{0,4},{4,8},{8,12},{1,5},{5,9},{9,13},{2,6},{6,10},{10,14},{3,7},{... | collective-permute-start | bytes 24584 | tf_op jit(solution)/shard_map/ppermute | solution.py:46
  228.4 8.0 %collective-permute-start.44 = (f32[4,64,1]{2,0,1:T(4,128)S(1)}, f32[4,64,1]{2,0,1:T(4,128)S(1)}, u32[]{:S(2)}, u32[]{:S(2)}) collective-permute-start(f32[4,64,1]{2,0,1:T(4,128)S(1)} %slice.963), channel_id=1, source_target_pairs={{0,16},{16,32},{32,48},{48,64},{64,80},{80,96},{96,112},{112,128},... | collective-permute-start | bytes 3080 | tf_op jit(solution)/shard_map/ppermute | solution.py:40
  238.8 16.0 %copy-start.5 = (f32[4,64,512]{2,0,1:T(4,128)}, f32[4,64,512]{2,0,1:T(4,128)S(1)}, u32[]{:S(2)}) copy-start(f32[4,64,512]{2,0,1:T(4,128)S(1)} %get-tuple-element.86) | copy-start | bytes 1572868
  238.8 16.0 %copy-start.7 = (f32[4,64,512]{2,0,1:T(4,128)}, f32[4,64,512]{2,0,1:T(4,128)S(1)}, u32[]{:S(2)}) copy-start(f32[4,64,512]{2,0,1:T(4,128)S(1)} %get-tuple-element.87) | copy-start | bytes 1572868
  239.0 8.9 %collective-permute-start.46 = (f32[2,4,64,1]{3,1,2,0:T(4,128)S(1)}, f32[2,4,64,1]{3,1,2,0:T(4,128)S(1)}, u32[]{:S(2)}, u32[]{:S(2)}) collective-permute-start(f32[2,4,64,1]{3,1,2,0:T(4,128)S(1)} %get-tuple-element.68), channel_id=1, source_target_pairs={{0,16},{16,32},{32,48},{48,64},{64,80},{80,96},{96,112},{112,128},... | collective-permute-start | bytes 6152 | tf_op jit(solution)/shard_map/ppermute | solution.py:31
  239.1 8.8 %collective-permute-start.47 = (f32[2,4,64,1]{3,1,2,0:T(4,128)S(1)}, f32[2,4,64,1]{3,1,2,0:T(4,128)S(1)}, u32[]{:S(2)}, u32[]{:S(2)}) collective-permute-start(f32[2,4,64,1]{3,1,2,0:T(4,128)S(1)} %get-tuple-element.69), channel_id=1, source_target_pairs={{16,0},{32,16},{48,32},{64,48},{80,64},{96,80},{112,96},{128,112},... | collective-permute-start | bytes 6152 | tf_op jit(solution)/shard_map/ppermute | solution.py:32
  248.0 3.5 collective-permute-start.48
  250.2 4.5 collective-permute-start.49
  257.1 11.4 %copy-start.3 = (f32[4,64,512]{2,0,1:T(4,128)}, f32[4,64,512]{2,0,1:T(4,128)S(1)}, u32[]{:S(2)}) copy-start(f32[4,64,512]{2,0,1:T(4,128)S(1)} %get-tuple-element.19) | copy-start | bytes 1572868
  259.0 35.9 %all-to-all-start = ((bf16[16,2,64,512]{3,2,1,0:T(8,128)(2,1)}), bf16[16,2,64,512]{3,2,1,0:T(8,128)(2,1)}, u32[]{:S(2)}, u32[]{:S(2)}) async-start(bf16[16,2,64,512]{3,2,1,0:T(8,128)(2,1)} %bitcast.187), calls=%async_computation | async-start | bytes 4194304 | tf_op jit(solution)/shard_map/all_to_all | solution.py:204
  265.8 373.6 %all-reduce.4.cloned.1.call-start = ((), (), s32[]{:S(2)}) async-start(), calls=%async_computation.1 | async-start | bytes 1417216 | tf_op jit(solution)/shard_map/psum | solution.py:225
  269.4 80.5 %collective-permute-start.51 = (f32[4,1,512]{2,0,1:T(4,128)}, f32[4,1,512]{2,0,1:T(4,128)}, u32[]{:S(2)}, u32[]{:S(2)}) collective-permute-start(f32[4,1,512]{2,0,1:T(4,128)} %slice.989), channel_id=1, source_target_pairs={{0,4},{4,8},{8,12},{1,5},{5,9},{9,13},{2,6},{6,10},{10,14},{3,7},{... | collective-permute-start | bytes 24584 | tf_op jit(solution)/shard_map/ppermute | solution.py:46
  271.9 78.0 %collective-permute-start.50 = (f32[4,64,1]{2,0,1:T(4,128)}, f32[4,64,1]{2,0,1:T(4,128)}, u32[]{:S(2)}, u32[]{:S(2)}) collective-permute-start(f32[4,64,1]{2,0,1:T(4,128)} %slice.983), channel_id=1, source_target_pairs={{0,16},{16,32},{32,48},{48,64},{64,80},{80,96},{96,112},{112,128},... | collective-permute-start | bytes 3080 | tf_op jit(solution)/shard_map/ppermute | solution.py:40
  342.1 7.8 %copy-start.2 = (f32[4,66,514]{2,0,1:T(4,128)S(1)}, f32[4,66,514]{2,0,1:T(4,128)}, u32[]{:S(2)}) copy-start(f32[4,66,514]{2,0,1:T(4,128)} %copy-done.1) | copy-start | bytes 1628356
  342.1 7.8 %copy-start.4 = (f32[4,64,512]{2,0,1:T(4,128)S(1)}, f32[4,64,512]{2,0,1:T(4,128)}, u32[]{:S(2)}) copy-start(f32[4,64,512]{2,0,1:T(4,128)} %copy-done.3) | copy-start | bytes 1572868
  342.1 7.8 %copy-start.6 = (f32[4,64,512]{2,0,1:T(4,128)S(1)}, f32[4,64,512]{2,0,1:T(4,128)}, u32[]{:S(2)}) copy-start(f32[4,64,512]{2,0,1:T(4,128)} %copy-done.5) | copy-start | bytes 1572868
  (9 other events, 29.3 us)
Sparse Core Ops, SparseCore 0:
  350.0 289.3 all-reduce.3
where the time goes:
time: 663 us; the launch traced here: 651 us
  waiting for transfers between devices  413 us (62%)
  starting transfers between devices  110 us (17%)
  local copies, waits for them, and re-layouts  57.4 us (9%)
  other arithmetic  44.2 us (7%)
  between operations  16.3 us (2%)
  matrix products  9.75 us (1%)
    psum x1, waiting for transfers between devices, shards(): grad_total = lax.psum(grad_local, ('lon', 'lat', 'grp'))  285 us
    ppermute x18, starting transfers between devices, extended(): after = lax.ppermute(initial, axis, down)  59.2 us
    ppermute x8, waiting for transfers between devices, passed_along(): return lax.ppermute(value, axis, pairs)  53.4 us
    ppermute x18, waiting for transfers between devices, extended(): before = lax.ppermute(last, axis, up)  27.6 us
    ppermute x18, waiting for transfers between devices, extended(): after = lax.ppermute(initial, axis, down)  26 us
    ppermute x18, starting transfers between devices, extended(): before = lax.ppermute(last, axis, up)  24.9 us
    all_to_all x1, waiting for transfers between devices, shards(): lax.all_to_all(blocks, 'lon', split_axis=0, concat_axis=3, tiled=True)[0]  21.5 us
    ppermute x8, starting transfers between devices, from_behind(): return lax.ppermute(block, axis, route)  17.4 us
  transfers between devices with their start and end apart: 54, of which 24 were waited for; matrix products, arithmetic and copies ran while one was open for 10% of the time, Pallas kernels for 0%

commit v1 on v0

v1 whole, which is shorter than its diff:
```python
import functools
import math

import jax
import jax.numpy as jnp
from jax import lax
from jax.experimental import pallas as pl
from jax.experimental.pallas import tpu as pltpu
from jax.sharding import PartitionSpec as P

STEPS = 8
NLEV = 50
PH = 8
PW = 16
GRAVITY = 0.45
DRAG_RATE = 0.02
CORI_BASE = 0.05
CORI_SLOPE = 0.1
WIND_SCALE = 0.05
EPSILON = 1e-06
HALF = 8
LANES = 128
F32 = jnp.float32
BF16 = jnp.bfloat16
PRECISE = lax.Precision.HIGHEST
MESH = pl.DeviceIdType.MESH
VMEM = pl.BlockSpec(memory_space=pltpu.VMEM)
SMEM = pl.BlockSpec(memory_space=pltpu.SMEM)


def iota(shape, dim):
    return lax.broadcasted_iota(jnp.int32, shape, dim)


def halo_kernel(
    ids_ref, prop_ref, sea_ref, vel_ref, lev_ref, wind_ref,
    frc_ref, rowf_ref, rowl_ref, colf_ref, coll_ref, corf_ref, corl_ref,
    east_ref, west_ref, send_sem, recv_sem,
):
    members, rows, cols = sea_ref.shape
    n_lon, n_lat = lax.axis_size("lon"), lax.axis_size("lat")
    lon, lat, grp = lax.axis_index("lon"), lax.axis_index("lat"), lax.axis_index("grp")
    east, west = lax.rem(lon + 1, n_lon), lax.rem(lon + n_lon - 1, n_lon)
    north, south = lax.rem(lat + 1, n_lat), lax.rem(lat + n_lat - 1, n_lat)

    barrier = pltpu.get_barrier_semaphore()
    for to_lat in (lat, north, south):
        for to_lon in (lon, east, west):
            if to_lat is lat and to_lon is lon:
                continue
            pl.semaphore_signal(
                barrier, inc=1, device_id={"lon": to_lon, "lat": to_lat}, device_id_type=MESH
            )

    coeffs = []
    for m in range(members):
        row = ids_ref[grp * members + m]
        for k in range(wind_ref.shape[0]):
            full = prop_ref[row, k]
            scaled = full * 65537.0
            coeffs.append(scaled - (scaled - full))

    def force(r, carry):
        at = pl.ds(pl.multiple_of(r * 16, 16), 16)
        total = [None] * members
        for k in range(wind_ref.shape[0]):
            wind = wind_ref[k, at, :].astype(F32)
            for m in range(members):
                term = coeffs[m * wind_ref.shape[0] + k] * wind
                total[m] = term if k == 0 else total[m] + term
        for m in range(members):
            frc_ref[m, at, :] = WIND_SCALE * total[m]
        return carry

    lax.fori_loop(0, rows // 16, force, 0)

    slot = iota((rows, LANES), 1) // 8
    fields = [(sea_ref, m) for m in range(members)]
    fields += [(vel_ref, m) for m in range(2 * members)]
    fields += [(frc_ref, m) for m in range(members)]
    pack_east = jnp.zeros((rows, LANES), F32)
    pack_west = jnp.zeros((rows, LANES), F32)
    for s, (ref, m) in enumerate(fields):
        right = ref[m, :, cols - LANES :]
        left = ref[m, :, :LANES]
        pack_east = jnp.where(slot == s, pltpu.roll(right, (8 * s + 8) % LANES, 1), pack_east)
        pack_west = jnp.where(slot == s, pltpu.roll(left, 8 * s, 1) if s else left, pack_west)
    east_ref[...] = pack_east
    west_ref[...] = pack_west

    pl.semaphore_wait(barrier, 8)

    copies = []

    def send(src, dst, to_lat, to_lon):
        i = len(copies)
        copy = pltpu.make_async_remote_copy(
            src_ref=src, dst_ref=dst, send_sem=send_sem.at[i], recv_sem=recv_sem.at[i],
            device_id={"lon": to_lon, "lat": to_lat}, device_id_type=MESH,
        )
        copy.start()
        copies.append(copy)

    for side, to_lat, first, wide in ((0, north, rows - 8, rows - 16), (1, south, 0, 0)):
        send(sea_ref.at[:, first : first + 8], rowf_ref.at[side, 0:members], to_lat, lon)
        send(vel_ref.at[:, first : first + 8], rowf_ref.at[side, members : 3 * members], to_lat, lon)
        send(frc_ref.at[:, first : first + 8], rowf_ref.at[side, 3 * members :], to_lat, lon)
        send(lev_ref.at[wide : wide + 16], rowl_ref.at[side], to_lat, lon)
    for side, to_lon, ref, first in ((0, east, east_ref, cols - LANES), (1, west, west_ref, 0)):
        send(ref, colf_ref.at[side], lat, to_lon)
        send(lev_ref.at[:, first : first + LANES], coll_ref.at[side], lat, to_lon)
    for side, to_lat, top, wide in ((0, north, rows - 8, rows - 16), (1, south, 0, 0)):
        for edge, to_lon, ref, first in ((0, east, east_ref, cols - LANES), (1, west, west_ref, 0)):
            send(ref.at[top : top + 8], corf_ref.at[2 * side + edge], to_lat, to_lon)
            send(
                lev_ref.at[wide : wide + 16, first : first + LANES],
                corl_ref.at[2 * side + edge], to_lat, to_lon,
            )
    for copy in copies:
        copy.wait()


def exchange_halos(ids, proposals, sea, vel, levels, wind):
    members, rows, cols = sea.shape
    slabs = 4 * members
    shape = jax.ShapeDtypeStruct
    return pl.pallas_call(
        halo_kernel,
        out_shape=(
            shape((members, rows, cols), F32),
            shape((2, slabs, 8, cols), F32),
            shape((2, 16, cols), jnp.int32),
            shape((2, rows, LANES), F32),
            shape((2, rows, LANES), jnp.int32),
            shape((4, 8, LANES), F32),
            shape((4, 16, LANES), jnp.int32),
        ),
        in_specs=[SMEM, SMEM, VMEM, VMEM, VMEM, VMEM],
        out_specs=(VMEM,) * 7,
        scratch_shapes=[
            pltpu.VMEM((rows, LANES), F32),
            pltpu.VMEM((rows, LANES), F32),
            pltpu.SemaphoreType.DMA((20,)),
            pltpu.SemaphoreType.DMA((20,)),
        ],
        compiler_params=pltpu.CompilerParams(collective_id=0, has_side_effects=True),
        name="halo",
    )(ids, proposals, sea, vel, levels, wind)


def block_transposed(tile):
    block = iota((8, LANES), 1) // PW
    tile = pltpu.roll(tile, 0, 1, stride=PW, stride_axis=0)
    for bit in (1, 2, 4):
        tile = jnp.where((block & bit) != 0, pltpu.roll(tile, 8 - bit, 0), tile)
    return pltpu.roll(tile, 0, 1, stride=PW, stride_axis=0)


def ocean_kernel(
    total_rows, total_cols, n_lon, place_ref, sea_ref, vel_ref, lev_ref, frc_ref, rowf_ref, rowl_ref, colf_ref, coll_ref,
    corf_ref, corl_ref, conv_ref, sea_out, vel_out, part_out, gram_out,
    state, hu_ref, hue_ref, hv_ref, hvu_ref, patches,
):
    members, rows, cols = sea_ref.shape
    slabs = 4 * members
    height, width = rows + 16, cols + LANES
    n_tiles = height // 8
    step = pl.program_id(0)
    lat = place_ref[0]
    inner_south = lat > 0
    inner_north = lat < total_rows // rows - 1

    @pl.when(step == 0)
    def _():
        low = iota((rows, LANES), 1) < 64
        low8 = iota((8, LANES), 1) < 64

        for s in range(slabs):
            if s < members:
                own = sea_ref[s]
            elif s < 3 * members:
                own = vel_ref[s - members]
            else:
                own = frc_ref[s - 3 * members]
            state[s, 8 : rows + 8, :cols] = own
            state[s, 0:8, :cols] = jnp.where(inner_south, rowf_ref[0, s], 0.0)
            state[s, rows + 8 :, :cols] = jnp.where(inner_north, rowf_ref[1, s], 0.0)

            def side(east_of, west_of, mask):
                return jnp.where(
                    mask, pltpu.roll(east_of, (LANES - 8 * s) % LANES, 1) if s else east_of,
                    pltpu.roll(west_of, (2 * LANES - 8 - 8 * s) % LANES, 1),
                )

            state[s, 8 : rows + 8, cols:] = side(colf_ref[1], colf_ref[0], low)
            state[s, 0:8, cols:] = jnp.where(inner_south, side(corf_ref[1], corf_ref[0], low8), 0.0)
            state[s, rows + 8 :, cols:] = jnp.where(
                inner_north, side(corf_ref[3], corf_ref[2], low8), 0.0
            )

        low16 = iota((16, LANES), 1) < 64
        south = jnp.concatenate(
            [rowl_ref[0], jnp.where(low16, corl_ref[1], corl_ref[0])], axis=1
        ).astype(F32)
        south = jnp.where(inner_south, south, 0.0)
        north = jnp.concatenate(
            [rowl_ref[1], jnp.where(low16, corl_ref[3], corl_ref[2])], axis=1
        ).astype(F32)
        north = jnp.where(inner_north, north, 0.0)
        own = jnp.concatenate([lev_ref[...], jnp.where(low, coll_ref[1], coll_ref[0])], axis=1).astype(F32)
        depth = jnp.concatenate([south, own, north], axis=0) / NLEV
        hu = 0.5 * (depth + pltpu.roll(depth, 1, 1))
        hue = pltpu.roll(hu, width - 1, 1)
        hv = 0.5 * (depth + pltpu.roll(depth, 1, 0))
        hvu = pltpu.roll(hv, rows + 31, 0)
        for ref, value in ((hu_ref, hu), (hue_ref, hue), (hv_ref, hv), (hvu_ref, hvu)):
            ref[...] = value[8 : height + 8]

    sub = iota((8, width), 0)
    first, last = sub == 0, sub == 7
    keep_south = jnp.where(inner_south, 1.0, 0.0)
    keep_north = jnp.where(inner_north, 1.0, 0.0)
    inv_root = 1.0 / math.sqrt(rows // PH * (total_cols // PW))
    per_dev = STEPS * members // n_lon

    def member(m, carry):
        n_cur = state[2 * members + m, 0:8, :]
        n_roll = pltpu.roll(n_cur, 7, 0)
        g_before = es_before = None
        held = []
        for k in range(n_tiles):
            at = slice(8 * k, 8 * k + 8)
            level = state[m, at, :]
            e = state[members + m, at, :]
            n = n_cur
            row = (lat * rows + (8 * k - 8) + iota((8, LANES), 0)).astype(F32)
            cu = 0.25 * (CORI_BASE + CORI_SLOPE * (row + 0.5) / total_rows)
            cv = 0.25 * (CORI_BASE + CORI_SLOPE * row / total_rows)
            cu = jnp.concatenate([cu] * (width // LANES), axis=1)
            cv = jnp.concatenate([cv] * (width // LANES), axis=1)
            if k + 1 < n_tiles:
                n_cur = state[2 * members + m, 8 * k + 8 : 8 * k + 16, :]
                n_next = pltpu.roll(n_cur, 7, 0)
                n_up = jnp.where(last, n_next, n_roll)
                n_roll = n_next
            else:
                n_up = n_roll
            e_e = pltpu.roll(e, width - 1, 1)
            new = level - (
                (hue_ref[at, :] * e_e - hu_ref[at, :] * e) + (hvu_ref[at, :] * n_up - hv_ref[at, :] * n)
            )
            keep = {0: keep_south, n_tiles - 1: keep_north}.get(k)
            if keep is not None:
                new = new * keep
            g = GRAVITY * new
            g_w = pltpu.roll(g, 1, 1)
            g_roll = pltpu.roll(g, 1, 0)
            g_s = g_roll if k == 0 else jnp.where(first, g_before, g_roll)
            g_before = g_roll
            ns = n + n_up
            v_sum = ns + pltpu.roll(ns, 1, 1)
            es = e + e_e
            es_roll = pltpu.roll(es, 1, 0)
            u_sum = es + (es_roll if k == 0 else jnp.where(first, es_before, es_roll))
            es_before = es_roll
            e_new = (1.0 - DRAG_RATE) * e + (cu * v_sum - (g - g_w) + state[3 * members + m, at, :])
            n_new = (1.0 - DRAG_RATE) * n - (cv * u_sum + (g - g_s))
            if keep is not None:
                e_new = e_new * keep
                n_new = n_new * keep
            state[m, at, :] = new
            state[members + m, at, :] = e_new
            state[2 * members + m, at, :] = n_new
            if 0 < k < n_tiles - 1:
                held.append(
                    [block_transposed(new[:, c * LANES : (c + 1) * LANES]) for c in range(cols // LANES)]
                )
                if len(held) == 2:
                    for c in range(cols // LANES):
                        i = (k // 2 - 1) * (cols // LANES) + c
                        patches[16 * i : 16 * i + 16, :] = jnp.concatenate(
                            [held[0][c], held[1][c]], axis=0
                        ).astype(BF16)
                    held = []

        cells = patches[...]
        act = jnp.tanh(jnp.dot(cells, conv_ref[...], preferred_element_type=F32))
        total = jnp.sum(act, axis=0, keepdims=True) * inv_root
        item = step * members + m
        part_out[item // per_dev, pl.ds(lax.rem(item, per_dev), 1), :] = total
        slope = 1.0 - act * act
        high = slope.astype(BF16)
        rest = (slope - high.astype(F32)).astype(BF16)
        over_rows = (((0,), (0,)), ((), ()))
        gram_out[m] = lax.dot_general(
            cells, high, over_rows, preferred_element_type=F32
        ) + lax.dot_general(cells, rest, over_rows, preferred_element_type=F32)
        return carry

    lax.fori_loop(0, members, member, 0)

    @pl.when(step == STEPS - 1)
    def _():
        for s in range(members):
            sea_out[s] = state[s, 8 : rows + 8, :cols]
        for s in range(2 * members):
            vel_out[s] = state[members + s, 8 : rows + 8, :cols]


def run_ocean(n_lon, n_lat, place, sea, vel, levels, halos, conv):
    members, rows, cols = sea.shape
    feat = conv.shape[1]
    height, width = rows + 16, cols + LANES
    per_dev = STEPS * members // n_lon
    shape = jax.ShapeDtypeStruct

    def whole(x):
        return pl.BlockSpec(x.shape, lambda t, *_: (0,) * len(x.shape), pipeline_mode=pl.Buffered(1))

    operands = (sea, vel, levels) + tuple(halos) + (conv,)
    outs = (
        shape(sea.shape, F32),
        shape(vel.shape, F32),
        shape((n_lon, per_dev, feat), F32),
        shape((STEPS * members, PH * PW, feat), F32),
    )
    return pl.pallas_call(
        functools.partial(ocean_kernel, rows * n_lat, cols * n_lon, n_lon),
        out_shape=outs,
        grid_spec=pltpu.PrefetchScalarGridSpec(
            num_scalar_prefetch=1,
            grid=(STEPS,),
            in_specs=[whole(x) for x in operands],
            out_specs=(
                whole(outs[0]),
                whole(outs[1]),
                whole(outs[2]),
                pl.BlockSpec((members, PH * PW, feat), lambda t, *_: (t, 0, 0)),
            ),
            scratch_shapes=[pltpu.VMEM((4 * members, height, width), F32)]
            + [pltpu.VMEM((height, width), F32)] * 4
            + [pltpu.VMEM((rows // PH * (cols // PW), PH * PW), BF16)],
        ),
        compiler_params=pltpu.CompilerParams(dimension_semantics=("arbitrary",)),
        name="ocean",
    )(place, *operands)


def precise(a, b, dims=(((1,), (0,)), ((), ()))):
    return lax.dot_general(a, b, dims, precision=PRECISE, preferred_element_type=F32)


def flow_gradients(params, summ, w_low, w_sum, b_in, w_out, b_out):
    lane = iota(params.shape, 1)
    hidden = jnp.tanh(precise(params, w_low) + precise(summ, w_sum) + b_in)
    raw = precise(hidden, w_out) + b_out
    log_scale = jnp.tanh(raw)
    scaled = pltpu.roll(params, LANES - HALF, 1) * jnp.exp(log_scale)
    latent = scaled + pltpu.roll(raw, LANES - HALF, 1)
    d_scale = (latent * scaled - 1.0) * (1.0 - log_scale * log_scale)
    d_raw = jnp.where(
        lane < HALF, d_scale, jnp.where(lane < 2 * HALF, pltpu.roll(latent, HALF, 1), 0.0)
    )
    d_hidden = precise(d_raw, w_out, (((1,), (1,)), ((), ()))) * (1.0 - hidden * hidden)
    return hidden, d_raw, d_hidden


def learn_kernel(
    inv_root, flat_size, ids_ref, prop_ref, part_ref, gram_ref, w_in_ref, b_in_ref, w_out_ref, b_out_ref, summary_ref, flat_ref,
    prop_pad, w_low, w_sum, w_out_pad, b_out_pad, near_sum, own_sum, lon_sum, all_sum, ds_ref,
    near_grad, got_grad, mid_own, mid_grad, end_own, end_grad, out_pad,
    send_sem, recv_sem,
):
    n_lon, per_dev, feat = part_ref.shape
    hid = w_in_ref.shape[1]
    n_lat, n_grp = lax.axis_size("lat"), lax.axis_size("grp")
    n_plane = n_lat * n_grp
    n_items = n_lon * per_dev
    n_members = prop_ref.shape[0]
    members = n_members // n_grp
    slice_rows = near_grad.shape[1]
    lon, lat, grp = lax.axis_index("lon"), lax.axis_index("lat"), lax.axis_index("grp")
    plane = lat * n_grp + grp

    def lon_peer(d):
        to = lax.rem(lon + d, n_lon)
        return to, {"lon": to}

    def plane_peer(d):
        to = lax.rem(plane + d, n_plane)
        return to, {"lat": to // n_grp, "grp": lax.rem(to, n_grp)}

    barrier = pltpu.get_barrier_semaphore()

    def greet(peer):
        def body(d, carry):
            pl.semaphore_signal(barrier, inc=1, device_id=peer(d)[1], device_id_type=MESH)
            return carry

        return body

    lax.fori_loop(1, n_lon, greet(lon_peer), 0)
    lax.fori_loop(1, n_plane, greet(plane_peer), 0)

    prop_pad[...] = jnp.zeros_like(prop_pad)
    prop_pad[:, : prop_ref.shape[1]] = prop_ref[...]
    w_low[...] = jnp.zeros_like(w_low)
    w_low[:HALF] = w_in_ref[:HALF]
    w_sum[...] = w_in_ref[HALF:]
    w_out_pad[...] = jnp.zeros_like(w_out_pad)
    w_out_pad[:, : 2 * HALF] = w_out_ref[...]
    b_out_pad[...] = jnp.zeros_like(b_out_pad)
    b_out_pad[:, : 2 * HALF] = b_out_ref[...]
    b_in, b_out = b_in_ref[...], b_out_pad[...]
    pick = (iota((n_members, n_members), 0) == ids_ref[...]).astype(F32)
    member_params = precise(pick, prop_pad[...], (((0,), (0,)), ((), ())))

    def params_of(n, group):
        inner = lax.rem(n, n_items)
        item = lax.rem(inner, n_lon) * per_dev + inner // n_lon
        chosen = group * members + lax.rem(item, members)
        return precise((chosen == iota(n.shape, 1)).astype(F32), member_params)

    n_near = iota((n_items, n_members), 0)
    near_params = params_of(n_near, grp)
    n_all = iota((n_plane * n_items, n_members), 0)
    all_params = params_of(n_all, lax.rem(n_all // n_items, n_grp))

    pl.semaphore_wait(barrier, n_lon + n_plane - 2)

    def exchange(phase, count, peer, source, target):
        def copy(d):
            to, device = peer(d)
            return pltpu.make_async_remote_copy(
                src_ref=source(to), dst_ref=target(d), send_sem=send_sem.at[phase, d],
                recv_sem=recv_sem.at[phase, d], device_id=device, device_id_type=MESH,
            )

        def start(d, carry):
            copy(d).start()
            return carry

        def finish(d, carry):
            copy(d).wait()
            return carry

        lax.fori_loop(1, count, start, 0)
        return lambda: lax.fori_loop(1, count, finish, 0)

    wait = exchange(0, n_lon, lon_peer, lambda to: part_ref.at[to], lambda d: near_sum.at[d])
    near_sum[0] = part_ref[lon]
    wait()
    total = near_sum[0]
    for d in range(1, n_lon):
        total = total + near_sum[d]
    own_sum[...] = total
    summary_ref[...] = total
    wait = exchange(1, n_lon, lon_peer, lambda to: own_sum, lambda d: lon_sum.at[lon])
    lon_sum[lon] = total
    wait()
    near = jnp.concatenate([lon_sum[:, q, :] for q in range(per_dev)], axis=0)
    all_sum[plane] = near
    wait_all = exchange(
        2, n_plane, plane_peer, lambda to: all_sum.at[plane], lambda d: all_sum.at[plane]
    )

    _, _, d_hidden = flow_gradients(near_params, near, w_low[...], w_sum[...], b_in, w_out_pad[...], b_out)
    ds_ref[...] = precise(d_hidden, w_sum[...], (((1,), (1,)), ((), ()))) * inv_root

    def accumulate(n, total):
        item = lax.rem(n, n_lon) * per_dev + n // n_lon
        return total + gram_ref[item] * ds_ref[pl.ds(n, 1), :]

    conv_grad = lax.fori_loop(0, n_items, accumulate, jnp.zeros(gram_ref.shape[1:], F32))
    near_grad[...] = conv_grad.reshape(near_grad.shape)
    wait = exchange(3, n_lon, lon_peer, lambda to: near_grad.at[to], lambda d: got_grad.at[d])

    wait_all()
    summ = all_sum[...].reshape(n_plane * n_items, feat)
    hidden, d_raw, d_hidden = flow_gradients(
        all_params, summ, w_low[...], w_sum[...], b_in, w_out_pad[...], b_out
    )

    got_grad[0] = near_grad[lon]
    wait()
    total = got_grad[0]
    for d in range(1, n_lon):
        total = total + got_grad[d]
    mid_own[...] = total
    wait = exchange(4, n_plane, plane_peer, lambda to: mid_own, lambda d: mid_grad.at[plane])
    mid_grad[plane] = total

    over_rows = (((0,), (0,)), ((), ()))
    conv_rows = PH * PW * feat // LANES
    wide = hid // LANES
    flat_ref[...] = jnp.zeros_like(flat_ref)
    g_low = precise(all_params, d_hidden, over_rows)[:HALF]
    g_sum = precise(summ, d_hidden, over_rows)
    for h in range(wide):
        flat_ref[pl.ds(conv_rows + h, HALF, stride=wide), :] = g_low[:, h * LANES : (h + 1) * LANES]
        flat_ref[pl.ds(conv_rows + HALF * wide + h, feat, stride=wide), :] = g_sum[:, h * LANES : (h + 1) * LANES]

    wait()
    total = mid_grad[0]
    for d in range(1, n_plane):
        total = total + mid_grad[d]
    end_own[...] = total
    wait = exchange(5, n_lon, lon_peer, lambda to: end_own, lambda d: end_grad.at[lon])
    end_grad[lon] = total

    base = conv_rows + (HALF + feat) * wide
    g_b_in = jnp.sum(d_hidden, axis=0, keepdims=True)
    for h in range(wide):
        flat_ref[base + h : base + h + 1, :] = g_b_in[:, h * LANES : (h + 1) * LANES]
    base += wide
    out_pad[...] = precise(hidden, d_raw, over_rows)
    per_row = LANES // (2 * HALF)
    out_rows = hid // per_row
    packed = out_pad[pl.ds(0, out_rows, stride=per_row), :]
    for s in range(1, per_row):
        packed = packed + pltpu.roll(
            out_pad[pl.ds(s, out_rows, stride=per_row), :], s * 2 * HALF, 1
        )
    flat_ref[base : base + out_rows, :] = packed
    base += out_rows
    flat_ref[base : base + 1, :] = jnp.sum(d_raw, axis=0, keepdims=True)

    wait()
    conv_grad = end_grad[...].reshape(PH * PW, feat)
    halves = feat // LANES
    for h in range(halves):
        flat_ref[pl.ds(h, PH * PW, stride=halves), :] = conv_grad[:, h * LANES : (h + 1) * LANES]
    flat = flat_ref[...]
    mean = jnp.sum(jnp.sum(flat * flat, axis=0, keepdims=True), axis=1, keepdims=True) / flat_size
    flat_ref[...] = flat * (-1.0 / jnp.sqrt(mean + EPSILON))


def learn(inv_root, ids, proposals, part, gram, w_in, b_in, w_out, b_out):
    n_lon, per_dev, feat = part.shape
    hid = w_in.shape[1]
    n_plane = lax.axis_size("lat") * lax.axis_size("grp")
    n_items = n_lon * per_dev
    cells = gram.shape[1]
    flat_size = cells * feat + w_in.size + b_in.size + w_out.size + b_out.size
    flat_rows = -(-flat_size // (8 * LANES)) * 8
    slice_rows = cells // n_lon
    piece = (slice_rows, feat)
    summary, flat = pl.pallas_call(
        functools.partial(learn_kernel, inv_root, float(flat_size)),
        out_shape=(
            jax.ShapeDtypeStruct((per_dev, feat), F32),
            jax.ShapeDtypeStruct((flat_rows, LANES), F32),
        ),
        in_specs=[VMEM] * 8,
        out_specs=(VMEM, VMEM),
        scratch_shapes=[
            pltpu.VMEM((proposals.shape[0], LANES), F32),
            pltpu.VMEM((LANES, hid), F32),
            pltpu.VMEM((feat, hid), F32),
            pltpu.VMEM((hid, LANES), F32),
            pltpu.VMEM((1, LANES), F32),
            pltpu.VMEM((n_lon, per_dev, feat), F32),
            pltpu.VMEM((per_dev, feat), F32),
            pltpu.VMEM((n_lon, per_dev, feat), F32),
            pltpu.VMEM((n_plane, n_items, feat), F32),
            pltpu.VMEM((n_items, feat), F32),
            pltpu.VMEM((n_lon,) + piece, F32),
            pltpu.VMEM((n_lon,) + piece, F32),
            pltpu.VMEM(piece, F32),
            pltpu.VMEM((n_plane,) + piece, F32),
            pltpu.VMEM(piece, F32),
            pltpu.VMEM((n_lon,) + piece, F32),
            pltpu.VMEM((hid, LANES), F32),
            pltpu.SemaphoreType.DMA((6, max(n_lon, n_plane))),
            pltpu.SemaphoreType.DMA((6, max(n_lon, n_plane))),
        ],
        compiler_params=pltpu.CompilerParams(collective_id=1, has_side_effects=True),
        name="learn",
    )(ids.reshape(1, -1), proposals, part, gram, w_in, b_in.reshape(1, -1), w_out, b_out.reshape(1, -1))
    return summary, flat.reshape(-1)[:flat_size]


def shards(
    sea_surface, velocity, levels, wind_basis, proposals, member_ids, conv_weight,
    couple_in, couple_in_bias, couple_out, couple_out_bias,
):
    members, rows, cols = sea_surface.shape
    n_lon, n_lat = lax.axis_size("lon"), lax.axis_size("lat")
    vel = velocity.reshape(2 * members, rows, cols)
    frc, *received = exchange_halos(member_ids, proposals, sea_surface, vel, levels, wind_basis)
    place = jnp.stack([lax.axis_index("lat"), lax.axis_index("lon")]).astype(jnp.int32)
    sea_out, vel_out, part, gram = run_ocean(
        n_lon, n_lat, place, sea_surface, vel, levels, (frc, *received), conv_weight
    )
    inv_root = 1.0 / math.sqrt(rows // PH * (cols * n_lon // PW))
    summary, weight_step = learn(
        inv_root, member_ids, proposals, part, gram, couple_in, couple_in_bias, couple_out, couple_out_bias
    )
    return (
        sea_out,
        vel_out.reshape(velocity.shape),
        summary.reshape((1, 1, 1) + summary.shape),
        weight_step,
    )


def solution(mesh):
    in_specs = (
        P("grp", "lat", "lon"),
        P(None, "grp", "lat", "lon"),
        P("lat", "lon"),
        P(None, "lat", "lon"),
        P(), P(), P(), P(), P(), P(), P(),
    )
    out_specs = (
        P("grp", "lat", "lon"),
        P(None, "grp", "lat", "lon"),
        P("lon", "lat", "grp", None, None),
        P(),
    )
    return jax.shard_map(shards, mesh=mesh, in_specs=in_specs, out_specs=out_specs, check_vma=False)
```

time: 663 us -> 100 us (0.15); the launches traced: 651 us -> 100 us
  waiting for transfers between devices: 413 us -> 0 us
  starting transfers between devices: 110 us -> 0 us
  Pallas kernels: 0 us -> 94.9 us
  local copies, waits for them, and re-layouts: 57.4 us -> 4.09 us
  other arithmetic: 44.2 us -> 0.59 us
  between operations: 16.3 us -> 0.66 us
  matrix products: 9.75 us -> 0 us
    psum x1 -> x0, waiting for transfers between devices: 285 us -> none  [shards(): grad_total = lax.psum(grad_local, ('lon', 'lat', 'grp'))]
    ppermute x52 -> x0, waiting for transfers between devices: 107 us -> none  [the longest x8 53.4 us: passed_along(): return lax.ppermute(value, axis, pairs)]
    ppermute x52 -> x0, starting transfers between devices: 104 us -> none  [the longest x18 59.2 us: extended(): after = lax.ppermute(initial, axis, down)]
    pallas_call x0 -> x3, Pallas kernels: none -> 94.9 us  [the longest x1 46.3 us: learn(): pl.pallas_call(functools.partial(learn_kernel, inv_root, float(flat_size)...]
    all_to_all x1 -> x0, waiting for transfers between devices: 21.5 us -> none  [shards(): lax.all_to_all(blocks, 'lon', split_axis=0, concat_axis=3, tiled=True)[0]]
    another operation x2 -> x0, local copies, waits for them, and re-layouts: 17.3 us -> none  [the longest x1 15.5 us: to_patches(): band_rows.reshape(count, height // kernel_rows, kernel_rows, breadth // k...]
    transpose x1 -> x0, local copies, waits for them, and re-layouts: 14.9 us -> none  [to_patches(): blocks.transpose(0, 1, 3, 2, 4).reshape(-1, kernel_rows * kernel_cols)]
    add x8 -> x0, other arithmetic: 14 us -> none  [the longest x6 13.9 us: velocity_update(): east_flow + cori_u * v_mean - GRAVITY * (new_level - west_level)]
  transfers between devices with their start and end apart: 54 -> 0, of which waited for: 24 -> 0; matrix products, arithmetic and copies ran while one was open for 10% -> 0% of each run, Pallas kernels for 0% -> 0%
where the time goes in v1:
time: 100 us
  Pallas kernels  94.9 us (95%)
  local copies, waits for them, and re-layouts  4.09 us (4%)
    pallas_call x1, Pallas kernels, learn(): pl.pallas_call(functools.partial(learn_kernel, inv_root, float(flat_size)...  46.3 us
    pallas_call x1, Pallas kernels, run_ocean(): pl.pallas_call(functools.partial(ocean_kernel, rows * n_lat, cols * n_lon...  27 us
    pallas_call x1, Pallas kernels, exchange_halos(): pl.pallas_call(halo_kernel, out_shape=(shape((members, rows, cols), F32),...  21.6 us
    unnamed x5, local copies, waits for them, and re-layouts  4.09 us

profile of v1, /device:TPU:1, one launch (start us, length us, event | category | flops | bytes accessed | tf_op | source)
XLA Modules:
  0.0 100.2 jit_solution(16170949726450321243)
XLA Ops:
  0.6 0.0 copy-start
  0.6 21.6 %halo.1 = (f32[4,64,512]{2,1,0:T(8,128)}, f32[2,16,8,512]{3,2,1,0:T(8,128)}, s32[2,16,512]{2,1,0:T(8,128)}, f32[2,64,128]{2,1,0:T(8,128)}, s32[2,64,128]{2,1,0:T...) custom-call(s32[16]{0:T(128)} %ids_ref.1, f32[16,16]{1,0:T(8,128)} %prop_ref.3, f32[4,64,512]{2,1,0:T(8,128)} %sea_ref.3, ...), custom_call_target="tpu_custom_call" | custom-call | tf_op jit(solution)/shard_map/halo/pallas_call | solution.py:127
  22.2 0.6 pad_add_fusion.place_ref
  22.8 27.0 %ocean.1 = (f32[4,64,512]{2,1,0:T(8,128)}, f32[8,64,512]{2,1,0:T(8,128)}, f32[16,2,256]{2,1,0:T(2,128)}, f32[32,128,256]{2,1,0:T(8,128)}) custom-call(s32[2]{0:T(128)} %pad_add_fusion.place_ref, f32[4,64,512]{2,1,0:T(8,128)} %sea_ref.3, f32[8,64,512]{2,1,0:T(8,128)} %bitcast.11, s32[64,512]{1,0:T(8,128)} %lev_ref.3, ...), custom_call_target="tpu_custom_call" | custom-call | tf_op jit(solution)/shard_map/ocean/pallas_call | solution.py:327
  49.8 0.0 copy-done
  49.8 0.8 copy.15.w_out_ref
  50.7 46.3 %learn.1 = (f32[2,256]{1,0:T(2,128)}, f32[1384,128]{1,0:T(8,128)}) custom-call(s32[1,16]{1,0:T(1,128)} %bitcast.14, f32[16,16]{1,0:T(8,128)} %prop_ref.3, f32[16,2,256]{2,1,0:T(2,128)} %get-tuple-element.26.part_ref, f32[32,128,256]{2,1,0:T(8,128)} %get-tuple-element.27.gram_ref, f32[264,512]{1,0:T(8,128)} %w_in_ref.1, f32[1,512]{1,0:T(1,128)} %bitcast.13, ...), custom_call_target="tpu_custom_call" | custom-call | tf_op jit(solution)/shard_map/learn/pallas_call | solution.py:548
  97.0 1.2 %copy.18 = f32[1,1,1,2,256]{4,3,2,1,0:T(2,128)} copy(f32[1,1,1,2,256]{4,3,2,1,0:T(2,128)} %bitcast.15) | data formatting | bytes 4096
  98.2 2.0 %copy.19 = f32[176656]{0:T(1024)} copy(f32[176656]{0:T(1024)} %bitcast.12) | data formatting | bytes 1413248
Async XLA Ops:
  0.6 49.2 %copy-start = (f32[512,16]{0,1:T(8,128)S(1)}, f32[512,16]{0,1:T(8,128)}, u32[]{:S(2)}) copy-start(f32[512,16]{0,1:T(8,128)} %param.20) | copy-start | bytes 98308

commit v2 on v0

v2 whole, which is shorter than its diff:
```python
import functools
import math

import jax
import jax.numpy as jnp
from jax import lax
from jax.experimental import pallas as pl
from jax.experimental.pallas import tpu as pltpu
from jax.sharding import PartitionSpec as P

STEPS = 8
NLEV = 50
PH = 8
PW = 16
GRAVITY = 0.45
DRAG_RATE = 0.02
CORI_BASE = 0.05
CORI_SLOPE = 0.1
WIND_SCALE = 0.05
EPSILON = 1e-06
HALF = 8
LANES = 128
F32 = jnp.float32
BF16 = jnp.bfloat16
PRECISE = lax.Precision.HIGHEST
MESH = pl.DeviceIdType.MESH
ANY = pl.BlockSpec(memory_space=pl.ANY)
VMEM = pl.BlockSpec(memory_space=pltpu.VMEM)
SMEM = pl.BlockSpec(memory_space=pltpu.SMEM)


def iota(shape, dim):
    return lax.broadcasted_iota(jnp.int32, shape, dim)


def block_transposed(tile):
    block = iota((8, LANES), 1) // PW
    tile = pltpu.roll(tile, 0, 1, stride=PW, stride_axis=0)
    for bit in (1, 2, 4):
        tile = jnp.where((block & bit) != 0, pltpu.roll(tile, 8 - bit, 0), tile)
    return pltpu.roll(tile, 0, 1, stride=PW, stride_axis=0)


def precise(a, b, dims=(((1,), (0,)), ((), ()))):
    return lax.dot_general(a, b, dims, precision=PRECISE, preferred_element_type=F32)


ROWS_OVER = (((0,), (0,)), ((), ()))
COLS_OVER = (((1,), (1,)), ((), ()))


def flow_gradients(params, summ, w_low, w_sum, b_in, w_out, b_out):
    lane = iota(params.shape, 1)
    hidden = jnp.tanh(precise(params, w_low) + precise(summ, w_sum) + b_in)
    raw = precise(hidden, w_out, COLS_OVER) + b_out
    log_scale = jnp.tanh(raw)
    scaled = pltpu.roll(params, LANES - HALF, 1) * jnp.exp(log_scale)
    latent = scaled + pltpu.roll(raw, LANES - HALF, 1)
    d_scale = (latent * scaled - 1.0) * (1.0 - log_scale * log_scale)
    d_raw = jnp.where(
        lane < HALF, d_scale, jnp.where(lane < 2 * HALF, pltpu.roll(latent, HALF, 1), 0.0)
    )
    d_hidden = precise(d_raw, w_out) * (1.0 - hidden * hidden)
    return hidden, d_raw, d_hidden


LEVEL, EAST, NORTH, FORCE = range(4)


def main_kernel(
    n_z, ids_s, prop_s, ids_ref, prop_ref, lev_ref, conv_ref, w_in_ref, b_in_ref, w_out_ref, b_out_ref,
    sea_ref, vel_ref, wind_ref,
    summary_ref, flat_ref, sea_out, vel_out,
    state, wind, hu_ref, hue_ref, hv_ref, hvu_ref, patches, gram, east_pack, west_pack,
    rowl_ref, colf_ref, coll_ref, corf_ref, corl_ref,
    prop_pad, w_low, w_sum, w_out_pad, b_out_pad, near_par, part, parts, all_sum, ds_ref,
    near_grad, got_grad, mid_grad, end_grad, out_pad,
    load_sem, store_sem, row_send, row_recv, edge_send, edge_recv, part_send, part_recv, sum_send, sum_recv,
    grad_send, grad_recv,
):
    members, _, height, width = state.shape
    rows, cols = height - 16, width - LANES
    n_lon, n_lat, n_grp = lax.axis_size("lon"), lax.axis_size("lat"), lax.axis_size("grp")
    lon, lat, grp = lax.axis_index("lon"), lax.axis_index("lat"), lax.axis_index("grp")
    total_rows, total_cols = rows * n_lat, cols * n_lon
    n_plane, n_hi = n_lat * n_grp, n_lon // n_z
    n_wide = n_hi * n_plane
    plane = lat * n_grp + grp
    hi, z = lon // n_z, lax.rem(lon, n_z)
    wide = hi * n_plane + plane
    n_members = prop_ref.shape[0]
    n_items = members * STEPS
    per_dev = n_items // n_lon
    feat = conv_ref.shape[1]
    hid = w_in_ref.shape[1]
    inv_root = 1.0 / math.sqrt(rows // PH * (total_cols // PW))
    own_rows, own_cols = slice(8, rows + 8), slice(0, cols)

    def lon_peer(d):
        to = lax.rem(lon + d, n_lon)
        return to, {"lon": to}

    def plane_peer(d):
        to = lax.rem(plane + d, n_plane)
        return to, {"lat": to // n_grp, "grp": lax.rem(to, n_grp)}

    def z_peer(d):
        to = lax.rem(z + d, n_z)
        return to, {"lon": hi * n_z + to}

    def wide_peer(d):
        to = lax.rem(wide + d, n_wide)
        rest = lax.rem(to, n_plane)
        return to, {"lon": (to // n_plane) * n_z + z, "lat": rest // n_grp, "grp": lax.rem(rest, n_grp)}

    east, west = lax.rem(lon + 1, n_lon), lax.rem(lon + n_lon - 1, n_lon)
    north, south = lax.rem(lat + 1, n_lat), lax.rem(lat + n_lat - 1, n_lat)

    barrier = pltpu.get_barrier_semaphore()
    for to_lat in (lat, north, south):
        for to_lon in (lon, east, west):
            if to_lat is lat and to_lon is lon:
                continue
            pl.semaphore_signal(
                barrier, inc=1, device_id={"lon": to_lon, "lat": to_lat}, device_id_type=MESH
            )

    def greet(peer):
        def body(d, carry):
            pl.semaphore_signal(barrier, inc=1, device_id=peer(d)[1], device_id_type=MESH)
            return carry

        return body

    lax.fori_loop(1, n_lon, greet(lon_peer), 0)
    lax.fori_loop(1, n_wide, greet(wide_peer), 0)

    loads = [
        pltpu.make_async_copy(wind_ref, wind, load_sem.at[0]),
        pltpu.make_async_copy(sea_ref, state.at[:, LEVEL, own_rows, own_cols], load_sem.at[1]),
        pltpu.make_async_copy(vel_ref.at[0], state.at[:, EAST, own_rows, own_cols], load_sem.at[2]),
        pltpu.make_async_copy(vel_ref.at[1], state.at[:, NORTH, own_rows, own_cols], load_sem.at[3]),
    ]
    for load in loads:
        load.start()

    coeffs = []
    for m in range(members):
        row = ids_s[grp * members + m]
        for k in range(wind_ref.shape[0]):
            full = prop_s[row, k]
            scaled = full * 65537.0
            coeffs.append(scaled - (scaled - full))

    loads[0].wait()

    def force(r, carry):
        at = pl.ds(pl.multiple_of(r * 16, 16), 16)
        total = [None] * members
        for k in range(wind_ref.shape[0]):
            blow = wind[k, at, :].astype(F32)
            for m in range(members):
                term = coeffs[m * wind_ref.shape[0] + k] * blow
                total[m] = term if k == 0 else total[m] + term
        for m in range(members):
            state[m, FORCE, pl.ds(pl.multiple_of(r * 16 + 8, 8), 16), own_cols] = WIND_SCALE * total[m]
        return carry

    lax.fori_loop(0, rows // 16, force, 0)
    for load in loads[1:]:
        load.wait()

    slot = iota((rows, LANES), 1) // 8
    east_edge = jnp.zeros((rows, LANES), F32)
    west_edge = jnp.zeros((rows, LANES), F32)
    for m in range(members):
        for f in range(4):
            s = 4 * m + f
            right = state[m, f, own_rows, cols - LANES : cols]
            left = state[m, f, own_rows, :LANES]
            east_edge = jnp.where(slot == s, pltpu.roll(right, (8 * s + 8) % LANES, 1), east_edge)
            west_edge = jnp.where(slot == s, pltpu.roll(left, 8 * s, 1) if s else left, west_edge)
    east_pack[...] = east_edge
    west_pack[...] = west_edge

    pl.semaphore_wait(barrier, 8 + n_lon - 1 + n_wide - 1)

    edges = []

    def send(src, dst, to_lat, to_lon):
        i = len(edges)
        copy = pltpu.make_async_remote_copy(
            src_ref=src, dst_ref=dst, send_sem=edge_send.at[i], recv_sem=edge_recv.at[i],
            device_id={"lon": to_lon, "lat": to_lat}, device_id_type=MESH,
        )
        copy.start()
        edges.append(copy)

    def row_copy(m, side):
        return pltpu.make_async_remote_copy(
            src_ref=state.at[m, :, (slice(rows, rows + 8), slice(8, 16))[side], own_cols],
            dst_ref=state.at[m, :, (slice(0, 8), slice(rows + 8, rows + 16))[side], own_cols],
            send_sem=row_send.at[m, side], recv_sem=row_recv.at[m, side],
            device_id={"lat": (north, south)[side]}, device_id_type=MESH,
        )

    for side, to_lat, wide_rows in ((0, north, slice(rows - 16, rows)), (1, south, slice(0, 16))):
        send(lev_ref.at[wide_rows], rowl_ref.at[side], to_lat, lon)
    for side, to_lon, ref, first in ((0, east, east_pack, cols - LANES), (1, west, west_pack, 0)):
        send(ref, colf_ref.at[side], lat, to_lon)
        send(lev_ref.at[:, first : first + LANES], coll_ref.at[side], lat, to_lon)
    for side in (0, 1):
        row_copy(0, side).start()
    for side, to_lat, top, wide_rows in (
        (0, north, rows - 8, slice(rows - 16, rows)), (1, south, 0, slice(0, 16)),
    ):
        for edge, to_lon, ref, first in ((0, east, east_pack, cols - LANES), (1, west, west_pack, 0)):
            send(ref.at[top : top + 8], corf_ref.at[2 * side + edge], to_lat, to_lon)
            send(
                lev_ref.at[wide_rows, first : first + LANES], corl_ref.at[2 * side + edge], to_lat, to_lon
            )
    for m in range(1, members):
        for side in (0, 1):
            row_copy(m, side).start()

    prop_pad[...] = jnp.zeros_like(prop_pad)
    prop_pad[:, : prop_ref.shape[1]] = prop_ref[...]
    w_low[...] = jnp.zeros_like(w_low)
    w_low[:HALF] = w_in_ref[:HALF]
    w_sum[...] = w_in_ref[HALF:]
    w_out_pad[...] = jnp.zeros_like(w_out_pad)
    w_out_pad[: 2 * HALF] = w_out_ref[...]
    b_out_pad[...] = jnp.zeros_like(b_out_pad)
    b_out_pad[:, : 2 * HALF] = b_out_ref[...]
    b_in, b_out = b_in_ref[...], b_out_pad[...]
    pick = (iota((n_members, n_members), 0) == ids_ref[...]).astype(F32)
    member_params = precise(pick, prop_pad[...], ROWS_OVER)

    def params_of(n, group):
        chosen = group * members + lax.rem(n, n_items) // STEPS
        return precise((chosen == iota(n.shape, 1)).astype(F32), member_params)

    near_par[...] = params_of(iota((n_items, n_members), 0), grp)

    for copy in edges:
        copy.wait()

    inner_south, inner_north = lat > 0, lat < n_lat - 1
    low = iota((rows, LANES), 1) < 64
    low8 = iota((8, LANES), 1) < 64
    for m in range(members):
        for f in range(4):
            s = 4 * m + f

            def beyond(east_of, west_of, mask):
                return jnp.where(
                    mask, pltpu.roll(east_of, (LANES - 8 * s) % LANES, 1) if s else east_of,
                    pltpu.roll(west_of, (2 * LANES - 8 - 8 * s) % LANES, 1),
                )

            state[m, f, own_rows, cols:] = beyond(colf_ref[1], colf_ref[0], low)
            state[m, f, 0:8, cols:] = beyond(corf_ref[1], corf_ref[0], low8)
            state[m, f, rows + 8 :, cols:] = beyond(corf_ref[3], corf_ref[2], low8)

    low16 = iota((16, LANES), 1) < 64
    below = jnp.concatenate([rowl_ref[0], jnp.where(low16, corl_ref[1], corl_ref[0])], axis=1).astype(F32)
    above = jnp.concatenate([rowl_ref[1], jnp.where(low16, corl_ref[3], corl_ref[2])], axis=1).astype(F32)
    own = jnp.concatenate([lev_ref[...], jnp.where(low, coll_ref[1], coll_ref[0])], axis=1).astype(F32)
    depth = jnp.concatenate(
        [jnp.where(inner_south, below, 0.0), own, jnp.where(inner_north, above, 0.0)], axis=0
    ) / NLEV
    hu = 0.5 * (depth + pltpu.roll(depth, 1, 1))
    hv = 0.5 * (depth + pltpu.roll(depth, 1, 0))
    for ref, value in (
        (hu_ref, hu), (hue_ref, pltpu.roll(hu, width - 1, 1)),
        (hv_ref, hv), (hvu_ref, pltpu.roll(hv, rows + 31, 0)),
    ):
        ref[...] = value[8 : height + 8]

    sub = iota((8, width), 0)
    first, last = sub == 0, sub == 7
    keep_south = jnp.where(inner_south, 1.0, 0.0)
    keep_north = jnp.where(inner_north, 1.0, 0.0)
    n_tiles = height // 8

    def advance(m, step):
        n_cur = state[m, NORTH, 0:8, :]
        n_roll = pltpu.roll(n_cur, 7, 0)
        g_before = es_before = None
        held = []
        for k in range(n_tiles):
            at = slice(8 * k, 8 * k + 8)
            e = state[m, EAST, at, :]
            n = n_cur
            row = (lat * rows + (8 * k - 8) + iota((8, LANES), 0)).astype(F32)
            cu = 0.25 * (CORI_BASE + CORI_SLOPE * (row + 0.5) / total_rows)
            cv = 0.25 * (CORI_BASE + CORI_SLOPE * row / total_rows)
            cu = jnp.concatenate([cu] * (width // LANES), axis=1)
            cv = jnp.concatenate([cv] * (width // LANES), axis=1)
            if k + 1 < n_tiles:
                n_cur = state[m, NORTH, 8 * k + 8 : 8 * k + 16, :]
                n_next = pltpu.roll(n_cur, 7, 0)
                n_up = jnp.where(last, n_next, n_roll)
                n_roll = n_next
            else:
                n_up = n_roll
            e_e = pltpu.roll(e, width - 1, 1)
            new = state[m, LEVEL, at, :] - (
                (hue_ref[at, :] * e_e - hu_ref[at, :] * e) + (hvu_ref[at, :] * n_up - hv_ref[at, :] * n)
            )
            keep = {0: keep_south, n_tiles - 1: keep_north}.get(k)
            if keep is not None:
                new = new * keep
            g = GRAVITY * new
            g_w = pltpu.roll(g, 1, 1)
            g_roll = pltpu.roll(g, 1, 0)
            g_s = g_roll if k == 0 else jnp.where(first, g_before, g_roll)
            g_before = g_roll
            ns = n + n_up
            v_sum = ns + pltpu.roll(ns, 1, 1)
            es = e + e_e
            es_roll = pltpu.roll(es, 1, 0)
            u_sum = es + (es_roll if k == 0 else jnp.where(first, es_before, es_roll))
            es_before = es_roll
            e_new = (1.0 - DRAG_RATE) * e + (cu * v_sum - (g - g_w) + state[m, FORCE, at, :])
            n_new = (1.0 - DRAG_RATE) * n - (cv * u_sum + (g - g_s))
            if keep is not None:
                e_new = e_new * keep
                n_new = n_new * keep
            state[m, LEVEL, at, :] = new
            state[m, EAST, at, :] = e_new
            state[m, NORTH, at, :] = n_new
            if 0 < k < n_tiles - 1:
                held.append(
                    [block_transposed(new[:, c * LANES : (c + 1) * LANES]) for c in range(cols // LANES)]
                )
                if len(held) == 2:
                    for c in range(cols // LANES):
                        i = (k // 2 - 1) * (cols // LANES) + c
                        patches[16 * i : 16 * i + 16, :] = jnp.concatenate(
                            [held[0][c], held[1][c]], axis=0
                        ).astype(BF16)
                    held = []

        cells = patches[...]
        act = jnp.tanh(jnp.dot(cells, conv_ref[...], preferred_element_type=F32))
        item = m * STEPS + step
        part[pl.ds(item, 1), :] = jnp.sum(act, axis=0, keepdims=True) * inv_root
        slope = 1.0 - act * act
        high = slope.astype(BF16)
        rest = (slope - high.astype(F32)).astype(BF16)
        gram[item] = lax.dot_general(
            cells, high, ROWS_OVER, preferred_element_type=F32
        ) + lax.dot_general(cells, rest, ROWS_OVER, preferred_element_type=F32)

    def exchange(count, peer, source, target, sends, recvs):
        def copy(d):
            to, device = peer(d)
            return pltpu.make_async_remote_copy(
                src_ref=source(to), dst_ref=target(d), send_sem=sends.at[d],
                recv_sem=recvs.at[d], device_id=device, device_id_type=MESH,
            )

        def start(d, carry):
            copy(d).start()
            return carry

        def finish(d, carry):
            copy(d).wait()
            return carry

        return (
            lambda: lax.fori_loop(1, count, start, 0),
            lambda: lax.fori_loop(1, count, finish, 0),
        )

    def group(m):
        return pl.ds(pl.multiple_of(m * STEPS, STEPS), STEPS)

    def share_parts(m):
        return exchange(
            n_lon, lon_peer, lambda to: part.at[group(m)], lambda d: parts.at[lon, group(m)],
            part_send.at[m], part_recv.at[m],
        )

    def share_sums(m):
        return exchange(
            n_plane, plane_peer, lambda to: all_sum.at[plane, group(m)], lambda d: all_sum.at[plane, group(m)],
            sum_send.at[m], sum_recv.at[m],
        )

    def summarize(m):
        share_parts(m)[1]()
        total = parts[0, group(m), :]
        for other in range(1, n_lon):
            total = total + parts[other, group(m), :]
        all_sum[plane, group(m), :] = total
        share_sums(m)[0]()

    def stores(m):
        own = (own_rows, own_cols)
        return [
            pltpu.make_async_copy(state.at[(m, LEVEL) + own], sea_out.at[m], store_sem.at[m, 0]),
            pltpu.make_async_copy(state.at[(m, EAST) + own], vel_out.at[0, m], store_sem.at[m, 1]),
            pltpu.make_async_copy(state.at[(m, NORTH) + own], vel_out.at[1, m], store_sem.at[m, 2]),
        ]

    def member(m, carry):
        for side in (0, 1):
            row_copy(m, side).wait()

        @pl.when(lat == 0)
        def _():
            state[m, :, 0:8, :] = jnp.zeros((4, 8, width), F32)

        @pl.when(lat == n_lat - 1)
        def _():
            state[m, :, rows + 8 :, :] = jnp.zeros((4, 8, width), F32)

        def one(step, inner):
            advance(m, step)
            return inner

        lax.fori_loop(0, STEPS, one, 0)
        for store in stores(m):
            store.start()
        parts[lon, group(m), :] = part[group(m), :]
        share_parts(m)[0]()

        @pl.when(m > 0)
        def _():
            summarize(m - 1)

        return carry

    lax.fori_loop(0, members, member, 0)

    def slopes(first_row, end_row, total):
        at = slice(first_row, end_row)
        _, _, d_hidden = flow_gradients(
            near_par[at], all_sum[plane, at, :], w_low[...], w_sum[...], b_in, w_out_pad[...], b_out
        )
        ds_ref[at] = precise(d_hidden, w_sum[...], COLS_OVER) * inv_root
        return lax.fori_loop(
            first_row, end_row, lambda j, acc: acc + gram[j] * ds_ref[pl.ds(j, 1), :], total
        )

    final = (members - 1) * STEPS
    conv_grad = slopes(0, final, jnp.zeros(gram.shape[1:], F32))
    summarize(members - 1)
    conv_grad = slopes(final, n_items, conv_grad)
    halves = feat // LANES
    for i in range(PH * PW // 8):
        for h in range(halves):
            near_grad[i * halves + h] = conv_grad[8 * i : 8 * i + 8, h * LANES : (h + 1) * LANES]
    per = near_grad.shape[0] // n_wide
    start, finish = exchange(
        n_wide, wide_peer, lambda to: near_grad.at[pl.ds(to * per, per)], lambda d: got_grad.at[d],
        grad_send.at[0], grad_recv.at[0],
    )
    start()

    for q in range(per_dev):
        item = lon * per_dev + q
        summary_ref[q : q + 1, :] = all_sum[
            plane, pl.ds(lax.rem(item, members) * STEPS + item // members, 1), :
        ]

    for m in range(members):
        share_sums(m)[1]()
    n_all = iota((n_plane * n_items, n_members), 0)
    all_params = params_of(n_all, lax.rem(n_all // n_items, n_grp))
    summ = all_sum[...].reshape(n_plane * n_items, feat)
    hidden, d_raw, d_hidden = flow_gradients(
        all_params, summ, w_low[...], w_sum[...], b_in, w_out_pad[...], b_out
    )

    got_grad[0] = near_grad[pl.ds(wide * per, per)]
    finish()
    total = got_grad[0]
    for d in range(1, n_wide):
        total = total + got_grad[d]
    mid_grad[z] = total
    start, finish = exchange(
        n_z, z_peer, lambda to: mid_grad.at[z], lambda d: mid_grad.at[z], grad_send.at[1], grad_recv.at[1]
    )
    start()

    conv_rows = PH * PW * feat // LANES
    w_cols = hid // LANES
    flat_ref[...] = jnp.zeros_like(flat_ref)
    g_low = precise(all_params, d_hidden, ROWS_OVER)[:HALF]
    g_sum = precise(summ, d_hidden, ROWS_OVER)
    for h in range(w_cols):
        flat_ref[pl.ds(conv_rows + h, HALF, stride=w_cols), :] = g_low[:, h * LANES : (h + 1) * LANES]
        flat_ref[pl.ds(conv_rows + HALF * w_cols + h, feat, stride=w_cols), :] = g_sum[
            :, h * LANES : (h + 1) * LANES
        ]

    finish()
    total = mid_grad[0]
    for d in range(1, n_z):
        total = total + mid_grad[d]
    mine = pl.ds(wide * per, per)
    end_grad[mine] = total
    start, finish = exchange(
        n_wide, wide_peer, lambda to: end_grad.at[mine], lambda d: end_grad.at[mine],
        grad_send.at[2], grad_recv.at[2],
    )
    start()

    base = conv_rows + (HALF + feat) * w_cols
    g_b_in = jnp.sum(d_hidden, axis=0, keepdims=True)
    for h in range(w_cols):
        flat_ref[base + h : base + h + 1, :] = g_b_in[:, h * LANES : (h + 1) * LANES]
    base += w_cols
    out_pad[...] = precise(hidden, d_raw, ROWS_OVER)
    per_row = LANES // (2 * HALF)
    out_rows = hid // per_row
    packed = out_pad[pl.ds(0, out_rows, stride=per_row), :]
    for s in range(1, per_row):
        packed = packed + pltpu.roll(
            out_pad[pl.ds(s, out_rows, stride=per_row), :], s * 2 * HALF, 1
        )
    flat_ref[base : base + out_rows, :] = packed
    base += out_rows
    flat_ref[base : base + 1, :] = jnp.sum(d_raw, axis=0, keepdims=True)
    for m in range(members):
        for store in stores(m):
            store.wait()

    finish()
    for i in range(PH * PW // 8):
        for h in range(halves):
            flat_ref[pl.ds(8 * i * halves + h, 8, stride=halves), :] = end_grad[i * halves + h]


def finish_kernel(flat_size, flat_ref, summary_ref, sea_ref, vel_ref, flat_out, summary_out, sea_out, vel_out, held, load_sem, store_sem):
    members = sea_ref.shape[0]
    sources = [sea_ref.at[m] for m in range(members)] + [vel_ref.at[i, m] for i in (0, 1) for m in range(members)]
    targets = [sea_out.at[m] for m in range(members)] + [vel_out.at[i, m] for i in (0, 1) for m in range(members)]
    loads = [pltpu.make_async_copy(src, held.at[i], load_sem.at[i]) for i, src in enumerate(sources)]
    stores = [pltpu.make_async_copy(held.at[i], dst, store_sem.at[i]) for i, dst in enumerate(targets)]
    for load in loads:
        load.start()
    for load, store in zip(loads, stores):
        load.wait()
        store.start()
    flat = flat_ref[...]
    mean = jnp.sum(jnp.sum(flat * flat, axis=0, keepdims=True), axis=1, keepdims=True) / flat_size
    flat_out[...] = flat * (-1.0 / jnp.sqrt(mean + EPSILON))
    summary_out[...] = summary_ref[...]
    for store in stores:
        store.wait()


def shards(
    sea_surface, velocity, levels, wind_basis, proposals, member_ids, conv_weight,
    couple_in, couple_in_bias, couple_out, couple_out_bias,
):
    members, rows, cols = sea_surface.shape
    n_lon, n_lat, n_grp = lax.axis_size("lon"), lax.axis_size("lat"), lax.axis_size("grp")
    n_z = n_lon // 2
    n_plane = n_lat * n_grp
    n_wide = n_lon // n_z * n_plane
    n_items = members * STEPS
    per_dev = n_items // n_lon
    cells, feat = conv_weight.shape
    hid = couple_in.shape[1]
    height, width = rows + 16, cols + LANES
    weights = (couple_in, couple_in_bias, couple_out, couple_out_bias)
    flat_size = cells * feat + sum(w.size for w in weights)
    flat_rows = -(-flat_size // (8 * LANES)) * 8
    pieces = cells // 8 * (feat // LANES)
    per = pieces // n_wide
    shape = jax.ShapeDtypeStruct
    vmem, dma = pltpu.VMEM, pltpu.SemaphoreType.DMA
    summary, flat, sea, vel = pl.pallas_call(
        functools.partial(main_kernel, n_z),
        out_shape=(
            shape((per_dev, feat), F32),
            shape((flat_rows, LANES), F32),
            shape(sea_surface.shape, F32),
            shape(velocity.shape, F32),
        ),
        in_specs=[SMEM] * 2 + [VMEM] * 8 + [ANY] * 3,
        out_specs=(VMEM, VMEM, ANY, ANY),
        scratch_shapes=[
            vmem((members, 4, height, width), F32),
            vmem(wind_basis.shape, BF16),
            vmem((height, width), F32),
            vmem((height, width), F32),
            vmem((height, width), F32),
            vmem((height, width), F32),
            vmem((rows // PH * (cols // PW), cells), BF16),
            vmem((n_items, cells, feat), F32),
            vmem((rows, LANES), F32),
            vmem((rows, LANES), F32),
            vmem((2, 16, cols), jnp.int32),
            vmem((2, rows, LANES), F32),
            vmem((2, rows, LANES), jnp.int32),
            vmem((4, 8, LANES), F32),
            vmem((4, 16, LANES), jnp.int32),
            vmem((proposals.shape[0], LANES), F32),
            vmem((LANES, hid), F32),
            vmem((feat, hid), F32),
            vmem((LANES, hid), F32),
            vmem((1, LANES), F32),
            vmem((n_items, LANES), F32),
            vmem((n_items, feat), F32),
            vmem((n_lon, n_items, feat), F32),
            vmem((n_plane, n_items, feat), F32),
            vmem((n_items, feat), F32),
            vmem((pieces, 8, LANES), F32),
            vmem((n_wide, per, 8, LANES), F32),
            vmem((n_z, per, 8, LANES), F32),
            vmem((pieces, 8, LANES), F32),
            vmem((hid, LANES), F32),
            dma((4,)),
            dma((members, 3)),
            dma((members, 2)),
            dma((members, 2)),
            dma((14,)),
            dma((14,)),
            dma((members, n_lon)),
            dma((members, n_lon)),
            dma((members, n_plane)),
            dma((members, n_plane)),
            dma((3, n_wide)),
            dma((3, n_wide)),
        ],
        compiler_params=pltpu.CompilerParams(collective_id=0, has_side_effects=True),
        name="ensemble",
    )(
        member_ids, proposals, member_ids.reshape(1, -1), proposals, levels, conv_weight, couple_in,
        couple_in_bias.reshape(1, -1), couple_out.T, couple_out_bias.reshape(1, -1),
        sea_surface, velocity, wind_basis,
    )
    flat, summary, sea, vel = pl.pallas_call(
        functools.partial(finish_kernel, float(flat_size)),
        out_shape=(
            shape(flat.shape, F32), shape(summary.shape, F32), shape(sea.shape, F32), shape(vel.shape, F32),
        ),
        in_specs=[VMEM, VMEM, ANY, ANY],
        out_specs=(VMEM, VMEM, ANY, ANY),
        scratch_shapes=[
            vmem((3 * members, rows, cols), F32),
            dma((3 * members,)),
            dma((3 * members,)),
        ],
        name="finish",
    )(flat, summary, sea, vel)
    return sea, vel, summary.reshape((1, 1, 1) + summary.shape), flat.reshape(-1)[:flat_size]


def solution(mesh):
    in_specs = (
        P("grp", "lat", "lon"),
        P(None, "grp", "lat", "lon"),
        P("lat", "lon"),
        P(None, "lat", "lon"),
        P(), P(), P(), P(), P(), P(), P(),
    )
    out_specs = (
        P("grp", "lat", "lon"),
        P(None, "grp", "lat", "lon"),
        P("lon", "lat", "grp", None, None),
        P(),
    )
    return jax.shard_map(shards, mesh=mesh, in_specs=in_specs, out_specs=out_specs, check_vma=False)
```

time: 663 us -> 80.8 us (0.12); the launches traced: 651 us -> 80.6 us
  waiting for transfers between devices: 413 us -> 0 us
  starting transfers between devices: 110 us -> 0 us
  Pallas kernels: 0 us -> 80 us
  local copies, waits for them, and re-layouts: 57.4 us -> 0 us
  other arithmetic: 44.2 us -> 0 us
  between operations: 16.3 us -> 0.64 us
  matrix products: 9.75 us -> 0 us
    psum x1 -> x0, waiting for transfers between devices: 285 us -> none  [shards(): grad_total = lax.psum(grad_local, ('lon', 'lat', 'grp'))]
    ppermute x52 -> x0, waiting for transfers between devices: 107 us -> none  [the longest x8 53.4 us: passed_along(): return lax.ppermute(value, axis, pairs)]
    ppermute x52 -> x0, starting transfers between devices: 104 us -> none  [the longest x18 59.2 us: extended(): after = lax.ppermute(initial, axis, down)]
    pallas_call x0 -> x2, Pallas kernels: none -> 80 us  [the longest x1 75.7 us: shards(): pl.pallas_call(functools.partial(main_kernel, n_z), out_shape=(shape((per...]
    all_to_all x1 -> x0, waiting for transfers between devices: 21.5 us -> none  [shards(): lax.all_to_all(blocks, 'lon', split_axis=0, concat_axis=3, tiled=True)[0]]
    another operation x2 -> x0, local copies, waits for them, and re-layouts: 17.3 us -> none  [the longest x1 15.5 us: to_patches(): band_rows.reshape(count, height // kernel_rows, kernel_rows, breadth // k...]
    transpose x1 -> x0, local copies, waits for them, and re-layouts: 14.9 us -> none  [to_patches(): blocks.transpose(0, 1, 3, 2, 4).reshape(-1, kernel_rows * kernel_cols)]
    add x8 -> x0, other arithmetic: 14 us -> none  [the longest x6 13.9 us: velocity_update(): east_flow + cori_u * v_mean - GRAVITY * (new_level - west_level)]
  transfers between devices with their start and end apart: 54 -> 0, of which waited for: 24 -> 0; matrix products, arithmetic and copies ran while one was open for 10% -> 0% of each run, Pallas kernels for 0% -> 0%
where the time goes in v2:
time: 80.8 us; the launch traced here: 80.6 us
  Pallas kernels  80 us (99%)
    pallas_call x1, Pallas kernels, shards(): pl.pallas_call(functools.partial(main_kernel, n_z), out_shape=(shape((per...  75.7 us
    pallas_call x1, Pallas kernels, shards(): pl.pallas_call(functools.partial(finish_kernel, float(flat_size)), out_sh...  4.29 us

profile of v2, /device:TPU:1, one launch (start us, length us, event | category | flops | bytes accessed | tf_op | source)
XLA Modules:
  0.0 80.6 jit_solution(18022751868496762698)
XLA Ops:
  0.6 75.7 %ensemble.1 = (f32[2,256]{1,0:T(2,128)}, f32[1384,128]{1,0:T(8,128)}, f32[4,64,512]{2,1,0:T(8,128)}, f32[2,4,64,512]{3,2,1,0:T(8,128)}) custom-call(s32[16]{0:T(128)} %ids_s.1, f32[16,16]{1,0:T(8,128)} %prop_ref.1, s32[1,16]{1,0:T(1,128)} %bitcast.9, f32[16,16]{1,0:T(8,128)} %prop_ref.1, s32[64,512]{1,0:T(8,128)} %lev_ref.1, bf16[128,256]{1,0:T(8,128)(2,1)} %conv_ref.1, ...), custom_call_target="tpu_custom_call" | custom-call | tf_op jit(solution)/shard_map/ensemble/pallas_call | solution.py:578
  76.3 4.3 %finish.1 = (f32[1384,128]{1,0:T(8,128)}, f32[2,256]{1,0:T(2,128)}, f32[4,64,512]{2,1,0:T(8,128)}, f32[2,4,64,512]{3,2,1,0:T(8,128)}) custom-call(f32[1384,128]{1,0:T(8,128)} %get-tuple-element.12.flat_ref, f32[2,256]{1,0:T(2,128)} %get-tuple-element.13.summary_ref, f32[4,64,512]{2,1,0:T(8,128)} %get-tuple-element.14.sea_ref, ...), custom_call_target="tpu_custom_call" | custom-call | tf_op jit(solution)/shard_map/finish/pallas_call | solution.py:639

commit v3 on v2

--- a/solution.py
+++ b/solution.py
@@ -22,7 +22,6 @@
 LANES = 128
 F32 = jnp.float32
 BF16 = jnp.bfloat16
-PRECISE = lax.Precision.HIGHEST
 MESH = pl.DeviceIdType.MESH
 ANY = pl.BlockSpec(memory_space=pl.ANY)
 VMEM = pl.BlockSpec(memory_space=pltpu.VMEM)
@@ -41,18 +40,28 @@
     return pltpu.roll(tile, 0, 1, stride=PW, stride_axis=0)
 
 
-def precise(a, b, dims=(((1,), (0,)), ((), ()))):
-    return lax.dot_general(a, b, dims, precision=PRECISE, preferred_element_type=F32)
-
-
 ROWS_OVER = (((0,), (0,)), ((), ()))
 COLS_OVER = (((1,), (1,)), ((), ()))
 
 
+def halves_of(x):
+    high = x.astype(BF16)
+    return high, (x - high.astype(F32)).astype(BF16)
+
+
+def product(a, b, dims=(((1,), (0,)), ((), ()))):
+    dot = functools.partial(lax.dot_general, dimension_numbers=dims, preferred_element_type=F32)
+    total = dot(a[0], b[0])
+    small = dot(a[0], b[1])
+    if len(a) > 1:
+        small = small + dot(a[1], b[0])
+    return total + small
+
+
 def flow_gradients(params, summ, w_low, w_sum, b_in, w_out, b_out):
     lane = iota(params.shape, 1)
-    hidden = jnp.tanh(precise(params, w_low) + precise(summ, w_sum) + b_in)
-    raw = precise(hidden, w_out, COLS_OVER) + b_out
+    hidden = jnp.tanh(product(halves_of(params), w_low) + product(summ, w_sum) + b_in)
+    raw = product(halves_of(hidden), w_out, COLS_OVER) + b_out
     log_scale = jnp.tanh(raw)
     scaled = pltpu.roll(params, LANES - HALF, 1) * jnp.exp(log_scale)
     latent = scaled + pltpu.roll(raw, LANES - HALF, 1)
@@ -60,7 +69,7 @@
     d_raw = jnp.where(
         lane < HALF, d_scale, jnp.where(lane < 2 * HALF, pltpu.roll(latent, HALF, 1), 0.0)
     )
-    d_hidden = precise(d_raw, w_out) * (1.0 - hidden * hidden)
+    d_hidden = product(halves_of(d_raw), w_out) * (1.0 - hidden * hidden)
     return hidden, d_raw, d_hidden
 
 
@@ -68,11 +77,11 @@
 
 
 def main_kernel(
-    n_z, ids_s, prop_s, ids_ref, prop_ref, lev_ref, conv_ref, w_in_ref, b_in_ref, w_out_ref, b_out_ref,
-    sea_ref, vel_ref, wind_ref,
+    n_z, ids_s, prop_s, ids_ref, prop_ref, lev_ref, conv_ref, b_in_ref, w_out_ref, b_out_ref,
+    sea_ref, vel_ref, wind_ref, w_in_ref,
     summary_ref, flat_ref, sea_out, vel_out,
-    state, wind, hu_ref, hue_ref, hv_ref, hvu_ref, patches, gram, east_pack, west_pack,
-    rowl_ref, colf_ref, coll_ref, corf_ref, corl_ref,
+    state, wind, w_in, hu_ref, hue_ref, hv_ref, hvu_ref, patches, gram, east_pack, west_pack, east_wind, west_wind,
+    rowl_ref, colf_ref, colw_ref, corf_ref, corw_ref,
     prop_pad, w_low, w_sum, w_out_pad, b_out_pad, near_par, part, parts, all_sum, ds_ref,
     near_grad, got_grad, mid_grad, end_grad, out_pad,
     load_sem, store_sem, row_send, row_recv, edge_send, edge_recv, part_send, part_recv, sum_send, sum_recv,
@@ -136,13 +145,71 @@
     lax.fori_loop(1, n_wide, greet(wide_peer), 0)
 
     loads = [
-        pltpu.make_async_copy(wind_ref, wind, load_sem.at[0]),
-        pltpu.make_async_copy(sea_ref, state.at[:, LEVEL, own_rows, own_cols], load_sem.at[1]),
-        pltpu.make_async_copy(vel_ref.at[0], state.at[:, EAST, own_rows, own_cols], load_sem.at[2]),
-        pltpu.make_async_copy(vel_ref.at[1], state.at[:, NORTH, own_rows, own_cols], load_sem.at[3]),
+        pltpu.make_async_copy(sea_ref, state.at[:, LEVEL, own_rows, own_cols], load_sem.at[0]),
+        pltpu.make_async_copy(vel_ref.at[0], state.at[:, EAST, own_rows, own_cols], load_sem.at[1]),
+        pltpu.make_async_copy(vel_ref.at[1], state.at[:, NORTH, own_rows, own_cols], load_sem.at[2]),
+        pltpu.make_async_copy(wind_ref, wind, load_sem.at[3]),
+        pltpu.make_async_copy(w_in_ref, w_in, load_sem.at[4]),
     ]
     for load in loads:
         load.start()
+    for load in loads[:3]:
+        load.wait()
+
+    slot = iota((rows, LANES), 1) // 8
+
+    def pack(packed, fields):
+        for s, (m, f) in enumerate(fields):
+            right = state[m, f, own_rows, cols - LANES : cols]
+            left = state[m, f, own_rows, :LANES]
+            packed = tuple(
+                jnp.where(slot == s, pltpu.roll(edge, shift, 1) if shift else edge, before)
+                for edge, shift, before in (
+                    (right, (8 * s + 8) % LANES, packed[0]), (left, 8 * s, packed[1]),
+                )
+            )
+        return packed
+
+    blank = jnp.zeros((rows, LANES), F32)
+    for ref, value in zip(
+        (east_pack, west_pack), pack((blank, blank), [(m, f) for m in range(members) for f in range(3)])
+    ):
+        ref[...] = value
+
+    pl.semaphore_wait(barrier, 8 + n_lon - 1 + n_wide - 1)
+
+    edges = []
+
+    def send(src, dst, to_lat, to_lon):
+        i = len(edges)
+        copy = pltpu.make_async_remote_copy(
+            src_ref=src, dst_ref=dst, send_sem=edge_send.at[i], recv_sem=edge_recv.at[i],
+            device_id={"lon": to_lon, "lat": to_lat}, device_id_type=MESH,
+        )
+        copy.start()
+        edges.append(copy)
+
+    top_rows, bottom_rows = (slice(rows, rows + 8), slice(8, 16)), (slice(0, 8), slice(rows + 8, rows + 16))
+
+    def row_copy(m, side):
+        return pltpu.make_async_remote_copy(
+            src_ref=state.at[m, LEVEL:FORCE, top_rows[side], own_cols],
+            dst_ref=state.at[m, LEVEL:FORCE, bottom_rows[side], own_cols],
+            send_sem=row_send.at[m, side], recv_sem=row_recv.at[m, side],
+            device_id={"lat": (north, south)[side]}, device_id_type=MESH,
+        )
+
+    def send_columns(packs, columns, corners, depth):
+        for side, to_lon in ((0, east), (1, west)):
+            send(packs[side], columns.at[side], lat, to_lon)
+        for side, to_lat, edge_rows in ((0, north, slice(rows - depth, rows)), (1, south, slice(0, depth))):
+            for edge, to_lon in ((0, east), (1, west)):
+                send(packs[edge].at[edge_rows], corners.at[2 * side + edge], to_lat, to_lon)
+
+    send_columns((east_pack, west_pack), colf_ref, corf_ref, 8)
+    for side, to_lat, wide_rows in ((0, north, slice(rows - 16, rows)), (1, south, slice(0, 16))):
+        send(lev_ref.at[wide_rows], rowl_ref.at[side], to_lat, lon)
+        row_copy(0, side).start()
 
     coeffs = []
     for m in range(members):
@@ -152,7 +219,7 @@
             scaled = full * 65537.0
             coeffs.append(scaled - (scaled - full))
 
-    loads[0].wait()
+    loads[3].wait()
 
     def force(r, carry):
         at = pl.ds(pl.multiple_of(r * 16, 16), 16)
@@ -167,78 +234,47 @@
         return carry
 
     lax.fori_loop(0, rows // 16, force, 0)
-    for load in loads[1:]:
-        load.wait()
-
-    slot = iota((rows, LANES), 1) // 8
-    east_edge = jnp.zeros((rows, LANES), F32)
-    west_edge = jnp.zeros((rows, LANES), F32)
-    for m in range(members):
-        for f in range(4):
-            s = 4 * m + f
-            right = state[m, f, own_rows, cols - LANES : cols]
-            left = state[m, f, own_rows, :LANES]
-            east_edge = jnp.where(slot == s, pltpu.roll(right, (8 * s + 8) % LANES, 1), east_edge)
-            west_edge = jnp.where(slot == s, pltpu.roll(left, 8 * s, 1) if s else left, west_edge)
-    east_pack[...] = east_edge
-    west_pack[...] = west_edge
-
-    pl.semaphore_wait(barrier, 8 + n_lon - 1 + n_wide - 1)
-
-    edges = []
-
-    def send(src, dst, to_lat, to_lon):
-        i = len(edges)
-        copy = pltpu.make_async_remote_copy(
-            src_ref=src, dst_ref=dst, send_sem=edge_send.at[i], recv_sem=edge_recv.at[i],
-            device_id={"lon": to_lon, "lat": to_lat}, device_id_type=MESH,
-        )
-        copy.start()
-        edges.append(copy)
-
-    def row_copy(m, side):
-        return pltpu.make_async_remote_copy(
-            src_ref=state.at[m, :, (slice(rows, rows + 8), slice(8, 16))[side], own_cols],
-            dst_ref=state.at[m, :, (slice(0, 8), slice(rows + 8, rows + 16))[side], own_cols],
-            send_sem=row_send.at[m, side], recv_sem=row_recv.at[m, side],
-            device_id={"lat": (north, south)[side]}, device_id_type=MESH,
-        )
-
-    for side, to_lat, wide_rows in ((0, north, slice(rows - 16, rows)), (1, south, slice(0, 16))):
-        send(lev_ref.at[wide_rows], rowl_ref.at[side], to_lat, lon)
-    for side, to_lon, ref, first in ((0, east, east_pack, cols - LANES), (1, west, west_pack, 0)):
-        send(ref, colf_ref.at[side], lat, to_lon)
-        send(lev_ref.at[:, first : first + LANES], coll_ref.at[side], lat, to_lon)
-    for side in (0, 1):
-        row_copy(0, side).start()
-    for side, to_lat, top, wide_rows in (
-        (0, north, rows - 8, slice(rows - 16, rows)), (1, south, 0, slice(0, 16)),
+    at_depth = (slot == members) | (slot == members + 1)
+    depth_east = pltpu.roll(lev_ref[:, cols - LANES :].astype(F32), 8 * members + 2 * 8, 1)
+    depth_west = pltpu.roll(lev_ref[:, :LANES].astype(F32), 8 * members, 1)
+    for ref, value in zip(
+        (east_wind, west_wind),
+        pack(
+            (jnp.where(at_depth, depth_east, 0.0), jnp.where(at_depth, depth_west, 0.0)),
+            [(m, FORCE) for m in range(members)],
+        ),
     ):
-        for edge, to_lon, ref, first in ((0, east, east_pack, cols - LANES), (1, west, west_pack, 0)):
-            send(ref.at[top : top + 8], corf_ref.at[2 * side + edge], to_lat, to_lon)
-            send(
-                lev_ref.at[wide_rows, first : first + LANES], corl_ref.at[2 * side + edge], to_lat, to_lon
-            )
+        ref[...] = value
+    send_columns((east_wind, west_wind), colw_ref, corw_ref, 16)
+    for side, to_lat in ((0, north), (1, south)):
+        send(
+            state.at[:, FORCE, top_rows[side], own_cols], state.at[:, FORCE, bottom_rows[side], own_cols],
+            to_lat, lon,
+        )
     for m in range(1, members):
         for side in (0, 1):
             row_copy(m, side).start()
 
+    loads[4].wait()
     prop_pad[...] = jnp.zeros_like(prop_pad)
     prop_pad[:, : prop_ref.shape[1]] = prop_ref[...]
-    w_low[...] = jnp.zeros_like(w_low)
-    w_low[:HALF] = w_in_ref[:HALF]
-    w_sum[...] = w_in_ref[HALF:]
-    w_out_pad[...] = jnp.zeros_like(w_out_pad)
-    w_out_pad[: 2 * HALF] = w_out_ref[...]
+
+    def padded(x):
+        return jnp.concatenate([x, jnp.zeros((LANES - x.shape[0], hid), F32)], axis=0)
+
+    for ref, value in (
+        (w_low, padded(w_in[:HALF])), (w_sum, w_in[HALF:]), (w_out_pad, padded(w_out_ref[...])),
+    ):
+        ref[0], ref[1] = halves_of(value)
     b_out_pad[...] = jnp.zeros_like(b_out_pad)
     b_out_pad[:, : 2 * HALF] = b_out_ref[...]
     b_in, b_out = b_in_ref[...], b_out_pad[...]
-    pick = (iota((n_members, n_members), 0) == ids_ref[...]).astype(F32)
-    member_params = precise(pick, prop_pad[...], ROWS_OVER)
+    pick = (iota((n_members, n_members), 0) == ids_ref[...]).astype(F32).astype(BF16)
+    member_params = halves_of(product((pick,), halves_of(prop_pad[...]), ROWS_OVER))
 
     def params_of(n, group):
         chosen = group * members + lax.rem(n, n_items) // STEPS
-        return precise((chosen == iota(n.shape, 1)).astype(F32), member_params)
+        return product(((chosen == iota(n.shape, 1)).astype(F32).astype(BF16),), member_params)
 
     near_par[...] = params_of(iota((n_items, n_members), 0), grp)
 
@@ -250,7 +286,7 @@
     low8 = iota((8, LANES), 1) < 64
     for m in range(members):
         for f in range(4):
-            s = 4 * m + f
+            s, columns, corners = (m, colw_ref, corw_ref) if f == FORCE else (3 * m + f, colf_ref, corf_ref)
 
             def beyond(east_of, west_of, mask):
                 return jnp.where(
@@ -258,14 +294,20 @@
                     pltpu.roll(west_of, (2 * LANES - 8 - 8 * s) % LANES, 1),
                 )
 
-            state[m, f, own_rows, cols:] = beyond(colf_ref[1], colf_ref[0], low)
-            state[m, f, 0:8, cols:] = beyond(corf_ref[1], corf_ref[0], low8)
-            state[m, f, rows + 8 :, cols:] = beyond(corf_ref[3], corf_ref[2], low8)
+            near_rows = slice(8, 16) if f == FORCE else slice(0, 8)
+            state[m, f, own_rows, cols:] = beyond(columns[1], columns[0], low)
+            state[m, f, 0:8, cols:] = beyond(corners[1, near_rows], corners[0, near_rows], low8)
+            state[m, f, rows + 8 :, cols:] = beyond(corners[3, 0:8], corners[2, 0:8], low8)
 
     low16 = iota((16, LANES), 1) < 64
-    below = jnp.concatenate([rowl_ref[0], jnp.where(low16, corl_ref[1], corl_ref[0])], axis=1).astype(F32)
-    above = jnp.concatenate([rowl_ref[1], jnp.where(low16, corl_ref[3], corl_ref[2])], axis=1).astype(F32)
-    own = jnp.concatenate([lev_ref[...], jnp.where(low, coll_ref[1], coll_ref[0])], axis=1).astype(F32)
+
+    def beside(east_of, west_of, mask):
+        shift = LANES - 8 * members
+        return jnp.where(mask, pltpu.roll(east_of, shift, 1), pltpu.roll(west_of, shift - 16, 1))
+
+    below = jnp.concatenate([rowl_ref[0].astype(F32), beside(corw_ref[1], corw_ref[0], low16)], axis=1)
+    above = jnp.concatenate([rowl_ref[1].astype(F32), beside(corw_ref[3], corw_ref[2], low16)], axis=1)
+    own = jnp.concatenate([lev_ref[...].astype(F32), beside(colw_ref[1], colw_ref[0], low)], axis=1)
     depth = jnp.concatenate(
         [jnp.where(inner_south, below, 0.0), own, jnp.where(inner_north, above, 0.0)], axis=0
     ) / NLEV
@@ -346,9 +388,7 @@
         act = jnp.tanh(jnp.dot(cells, conv_ref[...], preferred_element_type=F32))
         item = m * STEPS + step
         part[pl.ds(item, 1), :] = jnp.sum(act, axis=0, keepdims=True) * inv_root
-        slope = 1.0 - act * act
-        high = slope.astype(BF16)
-        rest = (slope - high.astype(F32)).astype(BF16)
+        high, rest = halves_of(1.0 - act * act)
         gram[item] = lax.dot_general(
             cells, high, ROWS_OVER, preferred_element_type=F32
         ) + lax.dot_general(cells, rest, ROWS_OVER, preferred_element_type=F32)
@@ -438,9 +478,9 @@
     def slopes(first_row, end_row, total):
         at = slice(first_row, end_row)
         _, _, d_hidden = flow_gradients(
-            near_par[at], all_sum[plane, at, :], w_low[...], w_sum[...], b_in, w_out_pad[...], b_out
-        )
-        ds_ref[at] = precise(d_hidden, w_sum[...], COLS_OVER) * inv_root
+            near_par[at], halves_of(all_sum[plane, at, :]), w_low, w_sum, b_in, w_out_pad, b_out
+        )
+        ds_ref[at] = product(halves_of(d_hidden), w_sum, COLS_OVER) * inv_root
         return lax.fori_loop(
             first_row, end_row, lambda j, acc: acc + gram[j] * ds_ref[pl.ds(j, 1), :], total
         )
@@ -470,10 +510,8 @@
         share_sums(m)[1]()
     n_all = iota((n_plane * n_items, n_members), 0)
     all_params = params_of(n_all, lax.rem(n_all // n_items, n_grp))
-    summ = all_sum[...].reshape(n_plane * n_items, feat)
-    hidden, d_raw, d_hidden = flow_gradients(
-        all_params, summ, w_low[...], w_sum[...], b_in, w_out_pad[...], b_out
-    )
+    summ = halves_of(all_sum[...].reshape(n_plane * n_items, feat))
+    hidden, d_raw, d_hidden = flow_gradients(all_params, summ, w_low, w_sum, b_in, w_out_pad, b_out)
 
     got_grad[0] = near_grad[pl.ds(wide * per, per)]
     finish()
@@ -489,8 +527,9 @@
     conv_rows = PH * PW * feat // LANES
     w_cols = hid // LANES
     flat_ref[...] = jnp.zeros_like(flat_ref)
-    g_low = precise(all_params, d_hidden, ROWS_OVER)[:HALF]
-    g_sum = precise(summ, d_hidden, ROWS_OVER)
+    d_halves = halves_of(d_hidden)
+    g_low = product(halves_of(all_params), d_halves, ROWS_OVER)[:HALF]
+    g_sum = product(summ, d_halves, ROWS_OVER)
     for h in range(w_cols):
         flat_ref[pl.ds(conv_rows + h, HALF, stride=w_cols), :] = g_low[:, h * LANES : (h + 1) * LANES]
         flat_ref[pl.ds(conv_rows + HALF * w_cols + h, feat, stride=w_cols), :] = g_sum[
@@ -514,7 +553,7 @@
     for h in range(w_cols):
         flat_ref[base + h : base + h + 1, :] = g_b_in[:, h * LANES : (h + 1) * LANES]
     base += w_cols
-    out_pad[...] = precise(hidden, d_raw, ROWS_OVER)
+    out_pad[...] = product(halves_of(hidden), halves_of(d_raw), ROWS_OVER)
     per_row = LANES // (2 * HALF)
     out_rows = hid // per_row
     packed = out_pad[pl.ds(0, out_rows, stride=per_row), :]
@@ -583,11 +622,12 @@
             shape(sea_surface.shape, F32),
             shape(velocity.shape, F32),
         ),
-        in_specs=[SMEM] * 2 + [VMEM] * 8 + [ANY] * 3,
+        in_specs=[SMEM] * 2 + [VMEM] * 7 + [ANY] * 4,
         out_specs=(VMEM, VMEM, ANY, ANY),
         scratch_shapes=[
             vmem((members, 4, height, width), F32),
             vmem(wind_basis.shape, BF16),
+            vmem(couple_in.shape, F32),
             vmem((height, width), F32),
             vmem((height, width), F32),
             vmem((height, width), F32),
@@ -596,15 +636,17 @@
             vmem((n_items, cells, feat), F32),
             vmem((rows, LANES), F32),
             vmem((rows, LANES), F32),
+            vmem((rows, LANES), F32),
+            vmem((rows, LANES), F32),
             vmem((2, 16, cols), jnp.int32),
             vmem((2, rows, LANES), F32),
-            vmem((2, rows, LANES), jnp.int32),
+            vmem((2, rows, LANES), F32),
             vmem((4, 8, LANES), F32),
-            vmem((4, 16, LANES), jnp.int32),
+            vmem((4, 16, LANES), F32),
             vmem((proposals.shape[0], LANES), F32),
-            vmem((LANES, hid), F32),
-            vmem((feat, hid), F32),
-            vmem((LANES, hid), F32),
+            vmem((2, LANES, hid), BF16),
+            vmem((2, feat, hid), BF16),
+            vmem((2, LANES, hid), BF16),
             vmem((1, LANES), F32),
             vmem((n_items, LANES), F32),
             vmem((n_items, feat), F32),
@@ -616,12 +658,12 @@
             vmem((n_z, per, 8, LANES), F32),
             vmem((pieces, 8, LANES), F32),
             vmem((hid, LANES), F32),
-            dma((4,)),
+            dma((5,)),
             dma((members, 3)),
             dma((members, 2)),
             dma((members, 2)),
-            dma((14,)),
-            dma((14,)),
+            dma((16,)),
+            dma((16,)),
             dma((members, n_lon)),
             dma((members, n_lon)),
             dma((members, n_plane)),
@@ -632,9 +674,9 @@
         compiler_params=pltpu.CompilerParams(collective_id=0, has_side_effects=True),
         name="ensemble",
     )(
-        member_ids, proposals, member_ids.reshape(1, -1), proposals, levels, conv_weight, couple_in,
+        member_ids, proposals, member_ids.reshape(1, -1), proposals, levels, conv_weight,
         couple_in_bias.reshape(1, -1), couple_out.T, couple_out_bias.reshape(1, -1),
-        sea_surface, velocity, wind_basis,
+        sea_surface, velocity, wind_basis, couple_in,
     )
     flat, summary, sea, vel = pl.pallas_call(
         functools.partial(finish_kernel, float(flat_size)),

time: 80.8 us -> 79.7 us (0.986)
  Pallas kernels: 80 us -> 78.9 us
    pallas_call x1, Pallas kernels: 75.7 us -> 74.6 us  [shards(): pl.pallas_call(functools.partial(main_kernel, n_z), out_shape=(shape((per...]
where the time goes in v3:
time: 79.7 us; the launch traced here: 79.6 us
  Pallas kernels  78.9 us (99%)
    pallas_call x1, Pallas kernels, shards(): pl.pallas_call(functools.partial(main_kernel, n_z), out_shape=(shape((per...  74.6 us
    pallas_call x1, Pallas kernels, shards(): pl.pallas_call(functools.partial(finish_kernel, float(flat_size)), out_sh...  4.29 us

profile of v3, /device:TPU:1, one launch (start us, length us, event | category | flops | bytes accessed | tf_op | source)
XLA Modules:
  0.0 79.6 jit_solution(6557960863057655139)
XLA Ops:
  0.6 74.6 %ensemble.1 = (f32[2,256]{1,0:T(2,128)}, f32[1384,128]{1,0:T(8,128)}, f32[4,64,512]{2,1,0:T(8,128)}, f32[2,4,64,512]{3,2,1,0:T(8,128)}) custom-call(s32[16]{0:T(128)} %ids_s.1, f32[16,16]{1,0:T(8,128)} %prop_ref.1, s32[1,16]{1,0:T(1,128)} %bitcast.9, f32[16,16]{1,0:T(8,128)} %prop_ref.1, s32[64,512]{1,0:T(8,128)} %lev_ref.1, bf16[128,256]{1,0:T(8,128)(2,1)} %conv_ref.1, ...), custom_call_target="tpu_custom_call" | custom-call | tf_op jit(solution)/shard_map/ensemble/pallas_call | solution.py:617
  75.3 4.3 %finish.1 = (f32[1384,128]{1,0:T(8,128)}, f32[2,256]{1,0:T(2,128)}, f32[4,64,512]{2,1,0:T(8,128)}, f32[2,4,64,512]{3,2,1,0:T(8,128)}) custom-call(f32[1384,128]{1,0:T(8,128)} %get-tuple-element.12.flat_ref, f32[2,256]{1,0:T(2,128)} %get-tuple-element.13.summary_ref, f32[4,64,512]{2,1,0:T(8,128)} %get-tuple-element.14.sea_ref, ...), custom_call_target="tpu_custom_call" | custom-call | tf_op jit(solution)/shard_map/finish/pallas_call | solution.py:681

commit v4 on v3

--- a/solution.py
+++ b/solution.py
@@ -74,6 +74,7 @@
 
 
 LEVEL, EAST, NORTH, FORCE = range(4)
+GROUP = 4
 
 
 def main_kernel(
@@ -325,7 +326,7 @@
     keep_north = jnp.where(inner_north, 1.0, 0.0)
     n_tiles = height // 8
 
-    def advance(m, step):
+    def advance(m, before):
         n_cur = state[m, NORTH, 0:8, :]
         n_roll = pltpu.roll(n_cur, 7, 0)
         g_before = es_before = None
@@ -384,16 +385,16 @@
                         ).astype(BF16)
                     held = []
 
+        item = before + 1
         cells = patches[...]
         act = jnp.tanh(jnp.dot(cells, conv_ref[...], preferred_element_type=F32))
-        item = m * STEPS + step
-        part[pl.ds(item, 1), :] = jnp.sum(act, axis=0, keepdims=True) * inv_root
+        part[item // GROUP, pl.ds(lax.rem(item, GROUP), 1)] = jnp.sum(act, axis=0, keepdims=True) * inv_root
         high, rest = halves_of(1.0 - act * act)
         gram[item] = lax.dot_general(
             cells, high, ROWS_OVER, preferred_element_type=F32
         ) + lax.dot_general(cells, rest, ROWS_OVER, preferred_element_type=F32)
 
-    def exchange(count, peer, source, target, sends, recvs):
+    def exchange(count, peer, source, target, sends, recvs, lead=1):
         def copy(d):
             to, device = peer(d)
             return pltpu.make_async_remote_copy(
@@ -402,11 +403,11 @@
             )
 
         def start(d, carry):
-            copy(d).start()
+            copy(1 + lax.rem(d + lead - 2, count - 1)).start()
             return carry
 
         def finish(d, carry):
-            copy(d).wait()
+            copy(1 + lax.rem(d + lead - 2, count - 1)).wait()
             return carry
 
         return (
@@ -417,10 +418,10 @@
     def group(m):
         return pl.ds(pl.multiple_of(m * STEPS, STEPS), STEPS)
 
-    def share_parts(m):
+    def share_parts(h):
         return exchange(
-            n_lon, lon_peer, lambda to: part.at[group(m)], lambda d: parts.at[lon, group(m)],
-            part_send.at[m], part_recv.at[m],
+            n_lon, lon_peer, lambda to: part.at[h], lambda d: parts.at[lon, h],
+            part_send.at[h], part_recv.at[h], 3 * n_lon // 4,
         )
 
     def share_sums(m):
@@ -429,13 +430,17 @@
             sum_send.at[m], sum_recv.at[m],
         )
 
-    def summarize(m):
-        share_parts(m)[1]()
-        total = parts[0, group(m), :]
+    def summarize(h):
+        share_parts(h)[1]()
+        total = parts[0, h]
         for other in range(1, n_lon):
-            total = total + parts[other, group(m), :]
-        all_sum[plane, group(m), :] = total
-        share_sums(m)[0]()
+            total = total + parts[other, h]
+        for r in range(GROUP):
+            all_sum[plane, pl.ds(h * GROUP + r, 1), :] = total[r : r + 1]
+
+        @pl.when(lax.rem(h, STEPS // GROUP) == STEPS // GROUP - 1)
+        def _():
+            share_sums(h // (STEPS // GROUP))[0]()
 
     def stores(m):
         own = (own_rows, own_cols)
@@ -445,36 +450,48 @@
             pltpu.make_async_copy(state.at[(m, NORTH) + own], vel_out.at[1, m], store_sem.at[m, 2]),
         ]
 
-    def member(m, carry):
-        for side in (0, 1):
-            row_copy(m, side).wait()
-
-        @pl.when(lat == 0)
+    n_groups = n_items // GROUP
+
+    def part_done(h):
+        parts[lon, h] = part[h]
+        share_parts(h)[0]()
+
+    def some_steps(h, carry):
+        m = h // (STEPS // GROUP)
+
+        @pl.when(lax.rem(h, STEPS // GROUP) == 0)
         def _():
-            state[m, :, 0:8, :] = jnp.zeros((4, 8, width), F32)
-
-        @pl.when(lat == n_lat - 1)
+            for side in (0, 1):
+                row_copy(m, side).wait()
+
+            @pl.when(lat == 0)
+            def _():
+                state[m, :, 0:8, :] = jnp.zeros((4, 8, width), F32)
+
+            @pl.when(lat == n_lat - 1)
+            def _():
+                state[m, :, rows + 8 :, :] = jnp.zeros((4, 8, width), F32)
+
+        def one(step, inner):
+            item = h * GROUP + step
+            advance(m, item - 1)
+            return inner
+
+        lax.fori_loop(0, GROUP, one, 0)
+
+        @pl.when(lax.rem(h, STEPS // GROUP) == STEPS // GROUP - 1)
         def _():
-            state[m, :, rows + 8 :, :] = jnp.zeros((4, 8, width), F32)
-
-        def one(step, inner):
-            advance(m, step)
-            return inner
-
-        lax.fori_loop(0, STEPS, one, 0)
-        for store in stores(m):
-            store.start()
-        parts[lon, group(m), :] = part[group(m), :]
-        share_parts(m)[0]()
-
-        @pl.when(m > 0)
+            for store in stores(m):
+                store.start()
+        part_done(h)
+
+        @pl.when(h > 0)
         def _():
-            summarize(m - 1)
+            summarize(h - 1)
 
         return carry
 
-    lax.fori_loop(0, members, member, 0)
-
+    lax.fori_loop(0, n_groups, some_steps, 0)
     def slopes(first_row, end_row, total):
         at = slice(first_row, end_row)
         _, _, d_hidden = flow_gradients(
@@ -485,9 +502,9 @@
             first_row, end_row, lambda j, acc: acc + gram[j] * ds_ref[pl.ds(j, 1), :], total
         )
 
-    final = (members - 1) * STEPS
+    final = n_items - 8
     conv_grad = slopes(0, final, jnp.zeros(gram.shape[1:], F32))
-    summarize(members - 1)
+    summarize(n_groups - 1)
     conv_grad = slopes(final, n_items, conv_grad)
     halves = feat // LANES
     for i in range(PH * PW // 8):
@@ -496,7 +513,7 @@
     per = near_grad.shape[0] // n_wide
     start, finish = exchange(
         n_wide, wide_peer, lambda to: near_grad.at[pl.ds(to * per, per)], lambda d: got_grad.at[d],
-        grad_send.at[0], grad_recv.at[0],
+        grad_send.at[0], grad_recv.at[0], 3 * n_wide // 4,
     )
     start()
 
@@ -544,7 +561,7 @@
     end_grad[mine] = total
     start, finish = exchange(
         n_wide, wide_peer, lambda to: end_grad.at[mine], lambda d: end_grad.at[mine],
-        grad_send.at[2], grad_recv.at[2],
+        grad_send.at[2], grad_recv.at[2], 3 * n_wide // 4,
     )
     start()
 
@@ -574,21 +591,29 @@
             flat_ref[pl.ds(8 * i * halves + h, 8, stride=halves), :] = end_grad[i * halves + h]
 
 
-def finish_kernel(flat_size, flat_ref, summary_ref, sea_ref, vel_ref, flat_out, summary_out, sea_out, vel_out, held, load_sem, store_sem):
+def finish_kernel(
+    flat_size, flat_ref, summary_ref, sea_ref, vel_ref, flat_out, summary_out, sea_out, vel_out,
+    flat, summary, held, load_sem, store_sem,
+):
     members = sea_ref.shape[0]
-    sources = [sea_ref.at[m] for m in range(members)] + [vel_ref.at[i, m] for i in (0, 1) for m in range(members)]
-    targets = [sea_out.at[m] for m in range(members)] + [vel_out.at[i, m] for i in (0, 1) for m in range(members)]
-    loads = [pltpu.make_async_copy(src, held.at[i], load_sem.at[i]) for i, src in enumerate(sources)]
-    stores = [pltpu.make_async_copy(held.at[i], dst, store_sem.at[i]) for i, dst in enumerate(targets)]
+    moves = [(flat_ref, flat, flat_out), (summary_ref, summary, summary_out)]
+    moves += [(sea_ref.at[m], held.at[m], sea_out.at[m]) for m in range(members)]
+    moves += [
+        (vel_ref.at[i, m], held.at[members * (i + 1) + m], vel_out.at[i, m])
+        for i in (0, 1) for m in range(members)
+    ]
+    loads = [pltpu.make_async_copy(a, b, load_sem.at[i]) for i, (a, b, _) in enumerate(moves)]
+    stores = [pltpu.make_async_copy(b, c, store_sem.at[i]) for i, (_, b, c) in enumerate(moves)]
     for load in loads:
         load.start()
-    for load, store in zip(loads, stores):
+    loads[0].wait()
+    total = flat[...]
+    mean = jnp.sum(jnp.sum(total * total, axis=0, keepdims=True), axis=1, keepdims=True) / flat_size
+    flat[...] = total * (-1.0 / jnp.sqrt(mean + EPSILON))
+    stores[0].start()
+    for load, store in zip(loads[1:], stores[1:]):
         load.wait()
         store.start()
-    flat = flat_ref[...]
-    mean = jnp.sum(jnp.sum(flat * flat, axis=0, keepdims=True), axis=1, keepdims=True) / flat_size
-    flat_out[...] = flat * (-1.0 / jnp.sqrt(mean + EPSILON))
-    summary_out[...] = summary_ref[...]
     for store in stores:
         store.wait()
 
@@ -633,7 +658,7 @@
             vmem((height, width), F32),
             vmem((height, width), F32),
             vmem((rows // PH * (cols // PW), cells), BF16),
-            vmem((n_items, cells, feat), F32),
+            vmem((n_items + 1, cells, feat), F32),
             vmem((rows, LANES), F32),
             vmem((rows, LANES), F32),
             vmem((rows, LANES), F32),
@@ -649,8 +674,8 @@
             vmem((2, LANES, hid), BF16),
             vmem((1, LANES), F32),
             vmem((n_items, LANES), F32),
-            vmem((n_items, feat), F32),
-            vmem((n_lon, n_items, feat), F32),
+            vmem((n_items // GROUP + 1, GROUP, feat), F32),
+            vmem((n_lon, n_items // GROUP, GROUP, feat), F32),
             vmem((n_plane, n_items, feat), F32),
             vmem((n_items, feat), F32),
             vmem((pieces, 8, LANES), F32),
@@ -664,8 +689,8 @@
             dma((members, 2)),
             dma((16,)),
             dma((16,)),
-            dma((members, n_lon)),
-            dma((members, n_lon)),
+            dma((n_items // GROUP, n_lon)),
+            dma((n_items // GROUP, n_lon)),
             dma((members, n_plane)),
             dma((members, n_plane)),
             dma((3, n_wide)),
@@ -683,12 +708,14 @@
         out_shape=(
             shape(flat.shape, F32), shape(summary.shape, F32), shape(sea.shape, F32), shape(vel.shape, F32),
         ),
-        in_specs=[VMEM, VMEM, ANY, ANY],
-        out_specs=(VMEM, VMEM, ANY, ANY),
+        in_specs=[ANY] * 4,
+        out_specs=(ANY,) * 4,
         scratch_shapes=[
+            vmem(flat.shape, F32),
+            vmem(summary.shape, F32),
             vmem((3 * members, rows, cols), F32),
-            dma((3 * members,)),
-            dma((3 * members,)),
+            dma((3 * members + 2,)),
+            dma((3 * members + 2,)),
         ],
         name="finish",
     )(flat, summary, sea, vel)

time: 79.7 us -> 89.9 us (1.13)
  Pallas kernels: 78.9 us -> 89.1 us
    pallas_call x1, Pallas kernels: 74.6 us -> 86.1 us  [shards(): pl.pallas_call(functools.partial(main_kernel, n_z), out_shape=(shape((per...]
    pallas_call x1, Pallas kernels: 4.29 us -> 3.04 us  [shards(): pl.pallas_call(functools.partial(finish_kernel, float(flat_size)), out_sh...]
where the time goes in v4:
time: 89.9 us; the launch traced here: 89.8 us
  Pallas kernels  89.1 us (99%)
    pallas_call x1, Pallas kernels, shards(): pl.pallas_call(functools.partial(main_kernel, n_z), out_shape=(shape((per...  86.1 us
    pallas_call x1, Pallas kernels, shards(): pl.pallas_call(functools.partial(finish_kernel, float(flat_size)), out_sh...  3.04 us

profile of v4, /device:TPU:1, one launch (start us, length us, event | category | flops | bytes accessed | tf_op | source)
XLA Modules:
  0.0 89.8 jit_solution(13148935595429683919)
XLA Ops:
  0.6 86.1 %ensemble.1 = (f32[2,256]{1,0:T(2,128)}, f32[1384,128]{1,0:T(8,128)}, f32[4,64,512]{2,1,0:T(8,128)}, f32[2,4,64,512]{3,2,1,0:T(8,128)}) custom-call(s32[16]{0:T(128)} %ids_s.1, f32[16,16]{1,0:T(8,128)} %prop_ref.1, s32[1,16]{1,0:T(1,128)} %bitcast.9, f32[16,16]{1,0:T(8,128)} %prop_ref.1, s32[64,512]{1,0:T(8,128)} %lev_ref.1, bf16[128,256]{1,0:T(8,128)(2,1)} %conv_ref.1, ...), custom_call_target="tpu_custom_call" | custom-call | tf_op jit(solution)/shard_map/ensemble/pallas_call | solution.py:642
  86.7 3.0 %finish.1 = (f32[1384,128]{1,0:T(8,128)}, f32[2,256]{1,0:T(2,128)}, f32[4,64,512]{2,1,0:T(8,128)}, f32[2,4,64,512]{3,2,1,0:T(8,128)}) custom-call(f32[1384,128]{1,0:T(8,128)} %get-tuple-element.12.flat_ref, f32[2,256]{1,0:T(2,128)} %get-tuple-element.13.summary_ref, f32[4,64,512]{2,1,0:T(8,128)} %get-tuple-element.14.sea_ref, ...), custom_call_target="tpu_custom_call" | custom-call | tf_op jit(solution)/shard_map/finish/pallas_call | solution.py:706

commit v5 on v4

--- a/solution.py
+++ b/solution.py
@@ -74,7 +74,8 @@
 
 
 LEVEL, EAST, NORTH, FORCE = range(4)
-GROUP = 4
+GROUP = 8
+LAG = 1
 
 
 def main_kernel(
@@ -394,7 +395,7 @@
             cells, high, ROWS_OVER, preferred_element_type=F32
         ) + lax.dot_general(cells, rest, ROWS_OVER, preferred_element_type=F32)
 
-    def exchange(count, peer, source, target, sends, recvs, lead=1):
+    def exchange(count, peer, source, target, sends, recvs):
         def copy(d):
             to, device = peer(d)
             return pltpu.make_async_remote_copy(
@@ -403,11 +404,11 @@
             )
 
         def start(d, carry):
-            copy(1 + lax.rem(d + lead - 2, count - 1)).start()
+            copy(d).start()
             return carry
 
         def finish(d, carry):
-            copy(1 + lax.rem(d + lead - 2, count - 1)).wait()
+            copy(d).wait()
             return carry
 
         return (
@@ -415,19 +416,19 @@
             lambda: lax.fori_loop(1, count, finish, 0),
         )
 
-    def group(m):
-        return pl.ds(pl.multiple_of(m * STEPS, STEPS), STEPS)
-
     def share_parts(h):
         return exchange(
             n_lon, lon_peer, lambda to: part.at[h], lambda d: parts.at[lon, h],
-            part_send.at[h], part_recv.at[h], 3 * n_lon // 4,
-        )
-
-    def share_sums(m):
+            part_send.at[h], part_recv.at[h],
+        )
+
+    shared = ((0, n_items - STEPS), (n_items - STEPS, n_items))
+
+    def share_sums(i):
+        at = slice(*shared[i])
         return exchange(
-            n_plane, plane_peer, lambda to: all_sum.at[plane, group(m)], lambda d: all_sum.at[plane, group(m)],
-            sum_send.at[m], sum_recv.at[m],
+            n_plane, plane_peer, lambda to: all_sum.at[plane, at], lambda d: all_sum.at[plane, at],
+            sum_send.at[i], sum_recv.at[i],
         )
 
     def summarize(h):
@@ -438,9 +439,10 @@
         for r in range(GROUP):
             all_sum[plane, pl.ds(h * GROUP + r, 1), :] = total[r : r + 1]
 
-        @pl.when(lax.rem(h, STEPS // GROUP) == STEPS // GROUP - 1)
-        def _():
-            share_sums(h // (STEPS // GROUP))[0]()
+        for i, (_, end) in enumerate(shared):
+            @pl.when(h == end // GROUP - 1)
+            def _():
+                share_sums(i)[0]()
 
     def stores(m):
         own = (own_rows, own_cols)
@@ -485,9 +487,9 @@
                 store.start()
         part_done(h)
 
-        @pl.when(h > 0)
+        @pl.when(h >= LAG)
         def _():
-            summarize(h - 1)
+            summarize(h - LAG)
 
         return carry
 
@@ -503,8 +505,11 @@
         )
 
     final = n_items - 8
+    for h in range(n_groups - LAG, final // GROUP):
+        summarize(h)
     conv_grad = slopes(0, final, jnp.zeros(gram.shape[1:], F32))
-    summarize(n_groups - 1)
+    for h in range(max(n_groups - LAG, final // GROUP), n_groups):
+        summarize(h)
     conv_grad = slopes(final, n_items, conv_grad)
     halves = feat // LANES
     for i in range(PH * PW // 8):
@@ -513,7 +518,7 @@
     per = near_grad.shape[0] // n_wide
     start, finish = exchange(
         n_wide, wide_peer, lambda to: near_grad.at[pl.ds(to * per, per)], lambda d: got_grad.at[d],
-        grad_send.at[0], grad_recv.at[0], 3 * n_wide // 4,
+        grad_send.at[0], grad_recv.at[0],
     )
     start()
 
@@ -523,8 +528,8 @@
             plane, pl.ds(lax.rem(item, members) * STEPS + item // members, 1), :
         ]
 
-    for m in range(members):
-        share_sums(m)[1]()
+    for i in range(len(shared)):
+        share_sums(i)[1]()
     n_all = iota((n_plane * n_items, n_members), 0)
     all_params = params_of(n_all, lax.rem(n_all // n_items, n_grp))
     summ = halves_of(all_sum[...].reshape(n_plane * n_items, feat))
@@ -561,7 +566,7 @@
     end_grad[mine] = total
     start, finish = exchange(
         n_wide, wide_peer, lambda to: end_grad.at[mine], lambda d: end_grad.at[mine],
-        grad_send.at[2], grad_recv.at[2], 3 * n_wide // 4,
+        grad_send.at[2], grad_recv.at[2],
     )
     start()
 
@@ -691,8 +696,8 @@
             dma((16,)),
             dma((n_items // GROUP, n_lon)),
             dma((n_items // GROUP, n_lon)),
-            dma((members, n_plane)),
-            dma((members, n_plane)),
+            dma((2, n_plane)),
+            dma((2, n_plane)),
             dma((3, n_wide)),
             dma((3, n_wide)),
         ],

time: 89.9 us -> 77.3 us (0.86)
  Pallas kernels: 89.1 us -> 76.6 us
    pallas_call x1, Pallas kernels: 86.1 us -> 73.5 us  [shards(): pl.pallas_call(functools.partial(main_kernel, n_z), out_shape=(shape((per...]
where the time goes in v5:
time: 77.3 us; the launch traced here: 77.2 us
  Pallas kernels  76.6 us (99%)
    pallas_call x1, Pallas kernels, shards(): pl.pallas_call(functools.partial(main_kernel, n_z), out_shape=(shape((per...  73.5 us
    pallas_call x1, Pallas kernels, shards(): pl.pallas_call(functools.partial(finish_kernel, float(flat_size)), out_sh...  3.04 us

profile of v5, /device:TPU:1, one launch (start us, length us, event | category | flops | bytes accessed | tf_op | source)
XLA Modules:
  0.0 77.2 jit_solution(8659810078548681139)
XLA Ops:
  0.6 73.5 %ensemble.1 = (f32[2,256]{1,0:T(2,128)}, f32[1384,128]{1,0:T(8,128)}, f32[4,64,512]{2,1,0:T(8,128)}, f32[2,4,64,512]{3,2,1,0:T(8,128)}) custom-call(s32[16]{0:T(128)} %ids_s.1, f32[16,16]{1,0:T(8,128)} %prop_ref.1, s32[1,16]{1,0:T(1,128)} %bitcast.9, f32[16,16]{1,0:T(8,128)} %prop_ref.1, s32[64,512]{1,0:T(8,128)} %lev_ref.1, bf16[128,256]{1,0:T(8,128)(2,1)} %conv_ref.1, ...), custom_call_target="tpu_custom_call" | custom-call | tf_op jit(solution)/shard_map/ensemble/pallas_call | solution.py:647
  74.2 3.0 %finish.1 = (f32[1384,128]{1,0:T(8,128)}, f32[2,256]{1,0:T(2,128)}, f32[4,64,512]{2,1,0:T(8,128)}, f32[2,4,64,512]{3,2,1,0:T(8,128)}) custom-call(f32[1384,128]{1,0:T(8,128)} %get-tuple-element.12.flat_ref, f32[2,256]{1,0:T(2,128)} %get-tuple-element.13.summary_ref, f32[4,64,512]{2,1,0:T(8,128)} %get-tuple-element.14.sea_ref, ...), custom_call_target="tpu_custom_call" | custom-call | tf_op jit(solution)/shard_map/finish/pallas_call | solution.py:711
